TPU v7x, 32 devices: a whole 2x2x4 slice. The times are simulated.
32 devices in a mesh: grp: 2 (over y), node: 4 (over z), sub: 2 (over x), rep: 2 (over core).
Axes of the slice: x: 2, y: 2, z: 4, core: 2. Of those that a mesh axis runs over, the one named last changes fastest.
Arguments:
- meson_nodes: float32 [2, 16, 512, 512], P(None, ('grp', 'node'), 'sub', 'rep'), parts along dimension 1, may hold values from -0.66 to 0.66
- term_nodes: int32 [8, 2], P('grp'), parts along dimension 0, may hold values from 0 to 7, as said below
- weight_codes: int32 [8], P('grp'), parts along dimension 0, may hold values from 0 to 7
- resident_pick: int32 [16], P('grp'), parts along dimension 0, may hold values from 0 to 1
Outputs:
- contracted: float32 [2, 16, 512, 512], P(None, ('grp', 'node'), 'sub', 'rep'), parts along dimension 1
There are 2 independent parts, one for each index of `grp`. A program takes and returns all parts, laid end to end along the dimension named above; each array names one. Nothing has to cross between parts.
Inputs may be any that keep to these rules, and one draw needn't show every extreme that they name: `term_nodes`: node n belongs to owner n // 2. In every term the two nodes differ. The first nodes of at most 2 terms belong to any one owner, and those of exactly 2 terms to some owner.
All inputs are finite; a program needn't handle non-finite values.
Results may differ from a plain program's by a relative error of at most 0.000098.
Values sent between devices are 32-bit elements; how exact they have to be, the bound alone decides.
A program may use at most 64 MiB of HBM per device.

v0:
```python
import functools

import jax
import jax.numpy as jnp
from jax import lax
from jax.experimental import pallas as pl
from jax.experimental.pallas import tpu as pltpu
from jax.sharding import PartitionSpec as P


def complex_step(full_left, segment):
    highest = lax.Precision.HIGHEST
    real_part = jnp.einsum(
        "kij,kjl->kil",
        full_left[0],
        segment[0],
        precision=highest,
        preferred_element_type=jnp.float32,
    ) - jnp.einsum(
        "kij,kjl->kil",
        full_left[1],
        segment[1],
        precision=highest,
        preferred_element_type=jnp.float32,
    )
    imag_part = jnp.einsum(
        "kij,kjl->kil",
        full_left[0],
        segment[1],
        precision=highest,
        preferred_element_type=jnp.float32,
    ) + jnp.einsum(
        "kij,kjl->kil",
        full_left[1],
        segment[0],
        precision=highest,
        preferred_element_type=jnp.float32,
    )
    return jnp.stack([real_part, imag_part])


def wide_body(meson_nodes, term_nodes, weight_codes, resident_pick):
    node_count = lax.axis_size("node")
    owned = meson_nodes.shape[1]
    row_count = meson_nodes.shape[2]
    col_count = meson_nodes.shape[3]
    band = row_count // node_count
    total_nodes = owned * node_count
    term_count = term_nodes.shape[0]
    banded = meson_nodes.reshape(2, owned, node_count, band * col_count)
    spread = lax.all_to_all(banded, "node", split_axis=2, concat_axis=1, tiled=True).reshape(
        2, total_nodes, band * col_count
    )
    leading = term_nodes[:, 0]
    trailing = term_nodes[:, 1]
    worker_ids = jnp.arange(node_count, dtype=jnp.int32)
    slot_count = term_count // node_count
    table = jnp.arange(slot_count, dtype=jnp.int32)[None, :] * node_count + worker_ids[:, None]
    active = jnp.ones(table.shape, jnp.float32)
    first_table = leading[table]
    second_table = trailing[table]
    factors = active * (weight_codes[table].astype(jnp.float32) - 3.5) * 0.5
    wanted = jnp.stack([first_table.T, second_table.T], axis=1)
    picked = jnp.take(spread, wanted, axis=1)
    fetched = lax.all_to_all(picked, "node", split_axis=3, concat_axis=3, tiled=True).reshape(
        2, slot_count, 2, row_count, col_count
    )
    left_rows = fetched[:, :, 0]
    right_band = fetched[:, :, 1]
    left_full = lax.all_gather(left_rows, "rep", axis=3, tiled=True)
    products = complex_step(left_full, lax.all_gather(right_band, "sub", axis=2, tiled=True))
    outgoing = products.reshape(2, slot_count, node_count, band * col_count)
    returned = lax.all_to_all(outgoing, "node", split_axis=2, concat_axis=1, tiled=True).reshape(
        2, node_count * slot_count, band * col_count
    )
    node_ids = jnp.arange(total_nodes, dtype=jnp.int32)
    incidence = (first_table.reshape(-1)[:, None] == node_ids[None, :]).astype(jnp.float32) + (
        second_table.reshape(-1)[:, None] == node_ids[None, :]
    ).astype(jnp.float32)
    mixing = factors.reshape(-1)[:, None] * incidence
    summed = jnp.einsum("mn,cmx->cnx", mixing, returned, precision=lax.Precision.HIGHEST)
    owner_sum = lax.all_to_all(
        summed.reshape(2, total_nodes, 1, band * col_count),
        "node",
        split_axis=1,
        concat_axis=2,
        tiled=True,
    ).reshape(2, owned, row_count, col_count)
    sum_full = lax.all_gather(owner_sum, "rep", axis=3, tiled=True)
    own_index = lax.axis_index("node")
    picks = lax.dynamic_slice_in_dim(resident_pick, own_index * owned, owned)
    resident = jnp.take(meson_nodes, picks, axis=1)
    return complex_step(sum_full, lax.all_gather(resident, "sub", axis=2, tiled=True))


MESH = pl.DeviceIdType.MESH
PIECES = 4
FOREIGN = 2


def split(value):
    high = value.astype(jnp.bfloat16)
    return high, (value - high.astype(jnp.float32)).astype(jnp.bfloat16)


def mul(left, right):
    def dot(p, q):
        return jnp.dot(p, q, preferred_element_type=jnp.float32)

    return dot(left[0], right[0]) + (dot(left[0], right[1]) + dot(left[1], right[0]))


def complex_mul(a0, a1, b0, b1):
    left, right = split(a0), split(b0)
    both = mul(left, right)
    left, right = split(a1), split(b1)
    other = mul(left, right)
    cross = mul(split(a0 + a1), split(b0 + b1))
    return both - other, cross - both - other


def line_kernel(
    length, owned, terms,
    x_ref, tn_ref, wc_ref, rp_ref, out_ref,
    nodes, rows, others, sums, picked,
    loc_sem, z_send, z_recv, c_send, c_recv, x_send, x_recv, s_send, s_recv,
):
    z = lax.axis_index("node")
    x = lax.axis_index("sub")
    c = lax.axis_index("rep")
    g = lax.axis_index("grp")
    left = (g, z - 1, x, c)
    right = (g, z + 1, x, c)
    across = (g, z, 1 - x, c)
    twin = (g, z, x, 1 - c)
    has_left = z > 0
    has_right = z < length - 1
    height = x_ref.shape[2] // PIECES
    pieces = [(j, m, r) for j in range(owned) for m in range(2) for r in range(PIECES)]

    def band(r):
        return pl.ds(r * height, height)

    def remote(src, dst, send, recv, device):
        return pltpu.make_async_remote_copy(
            src_ref=src, dst_ref=dst, send_sem=send, recv_sem=recv, device_id=device, device_id_type=MESH
        )

    barrier = pltpu.get_barrier_semaphore()
    for device in (across, twin):
        pl.semaphore_signal(barrier, inc=1, device_id=device, device_id_type=MESH)

    @pl.when(has_left)
    def _():
        pl.semaphore_signal(barrier, inc=1, device_id=left, device_id_type=MESH)

    @pl.when(has_right)
    def _():
        pl.semaphore_signal(barrier, inc=1, device_id=right, device_id_type=MESH)

    pl.semaphore_wait(barrier, 2 + has_left.astype(jnp.int32) + has_right.astype(jnp.int32))

    def node_at(owner, j, m, r):
        return nodes.at[c, owner * owned + j, m, band(r)]

    def own_at(j, m, r):
        return x_ref.at[m, j, band(r)]

    def reach(way, step):
        return z + step if way == 0 else z - step

    def inside(owner):
        return jnp.logical_and(owner >= 0, owner <= length - 1)

    def to_end(way):
        return z == (1 if way == 0 else length - 2)

    def z_sends(way, step):
        found = jnp.logical_and(has_left if way == 0 else has_right, inside(reach(way, step)))
        return jnp.logical_and(found, jnp.logical_not(to_end(way))) if step == 0 else found

    def z_arrives(way, step):
        found = inside(reach(way, step + 1))
        return jnp.logical_and(found, z != (0 if way == 0 else length - 1)) if step == 0 else found

    def z_copy(way, step, j, m, r, src):
        return remote(
            src, node_at(reach(way, step), j, m, r), z_send.at[way, step, j, m, r],
            z_recv.at[way, step, j, m, r], left if way == 0 else right,
        )

    def c_copy(owner, j, m, r, src):
        return remote(
            src, node_at(owner, j, m, r), c_send.at[owner, j, m, r], c_recv.at[owner, j, m, r], twin
        )

    def x_copy(k, m, r, src):
        return remote(src, others.at[k, m, band(r)], x_send.at[k, m, r], x_recv.at[k, m, r], across)

    def s_copy(h, j, m):
        return remote(sums.at[h, j, m], sums.at[h, j, m], s_send.at[j, m], s_recv.at[j, m], twin)

    for way in range(2):

        @pl.when(z_sends(way, 0))
        def _():
            for piece in pieces:
                z_copy(way, 0, *piece, own_at(*piece)).start()

    for piece in pieces:
        x_copy(*piece, own_at(*piece)).start()
    local = []
    for j, m, r in pieces:
        for i, dst in enumerate((node_at(z, j, m, r), rows.at[j, m, band(r)])):
            copy = pltpu.make_async_copy(own_at(j, m, r), dst, loc_sem.at[i, j, m, r])
            copy.start()
            local.append(copy)
        c_copy(z, j, m, r, own_at(j, m, r)).start()

    firsts = [tn_ref[0, t] for t in range(terms)]
    seconds = [tn_ref[1, t] for t in range(terms)]
    spots = (length - 2) * owned

    def holds(owner, n):
        return jnp.logical_and(n >= owner * owned, n < owner * owned + owned)

    def rank_of(end, n):
        owner = n // owned
        return jnp.where(end == 0, owner, length - 1 - owner) * owned + n - owner * owned

    def node_of(end, rank):
        far = rank // owned
        return jnp.where(end == 0, far, length - 1 - far) * owned + rank % owned

    def partner_ranks(end):
        ranks = []
        for a, b in zip(firsts, seconds):
            here, there = holds(end, a), holds(end, b)
            rank = jnp.where(here, rank_of(end, b), rank_of(end, a))
            ranks.append(jnp.where(here != there, rank, owned))
        below, found = length * owned, []
        for _ in range(spots):
            best = owned
            for rank in ranks:
                best = jnp.where(jnp.logical_and(rank < below, rank > best), rank, best)
            found.append(best)
            below = best
        return found[::-1]

    end = jnp.where(z < length // 2, 0, length - 1)
    wanted_ranks = partner_ranks(end)
    at_end = z == end

    def entry(n):
        place = z * owned
        rank = rank_of(end, n)
        for i in range(spots):
            place = jnp.where(wanted_ranks[i] == rank, node_of(end, 2 * owned + i), place)
        return jnp.where(jnp.logical_and(at_end, jnp.logical_not(holds(z, n))), place, n)

    far = length - 1 - end
    late = far * owned + owned - 1
    home = z * owned
    left_entries = [entry(a) for a in firsts]
    right_entries = [entry(b) for b in seconds]
    needs = [
        jnp.logical_and(holds(z, a), jnp.logical_not(holds(z, b))) for a, b in zip(firsts, seconds)
    ]
    slot1 = home
    for need, e in zip(needs, right_entries):
        slot1 = jnp.where(jnp.logical_and(need, slot1 != late), e, slot1)
    slot0 = home
    for need, e in zip(needs, right_entries):
        slot0 = jnp.where(jnp.logical_and(need, e != slot1), e, slot0)

    for copy in local:
        copy.wait()

    def pick(i, m, r):
        chosen = nodes[c, node_of(end, owned), m, band(r)]
        for rank in range(owned + 1, 2 * owned + i + 1):
            chosen = jnp.where(
                wanted_ranks[i] == rank, nodes[c, node_of(end, rank), m, band(r)], chosen
            )
        picked[i, m, band(r)] = chosen

    def stage(s, m, r):
        wanted = slot1 if s else slot0
        chosen = nodes[c, home, m, band(r)]
        for k in range(length):
            owner = lax.rem(far + 1 + k, length)
            for j in range(owned):
                if s == 0 and k == length - 1 and j == owned - 1:
                    continue
                n = owner * owned + j
                chosen = jnp.where(wanted == n, nodes[c, n, m, band(r)], chosen)
        rows[owned + s, m, band(r)] = chosen
        x_copy(owned + s, m, r, rows.at[owned + s, m, band(r)]).start()

    depth = jnp.maximum(z, length - 1 - z) - 1
    for step in range(length - 1):
        for j, m, r in pieces:
            for way in range(2):

                @pl.when(z_arrives(way, step))
                def _():
                    owner = reach(way, step + 1)
                    src = node_at(owner, j, m, r)
                    remote(
                        src, src, z_send.at[way, step, j, m, r], z_recv.at[way, step, j, m, r],
                        left if way == 0 else right,
                    ).wait_recv()
                    c_copy(owner, j, m, r, src).start()

                if step < length - 2:
                    goes = jnp.logical_and(z_arrives(way, step), z_sends(way, step + 1))

                    @pl.when(jnp.logical_and(goes, jnp.logical_not(to_end(way))))
                    def _():
                        z_copy(way, step + 1, j, m, r, node_at(reach(way, step + 1), j, m, r)).start()

                    @pl.when(jnp.logical_and(goes, to_end(way)))
                    def _():
                        i = step * owned + j
                        pick(i, m, r)
                        z_copy(way, step + 1, j, m, r, picked.at[i, m, band(r)]).start()

            if step >= length // 2 - 1:

                @pl.when(depth == step)
                def _():
                    stage(j, m, r)

    def filled(owner):
        beside = jnp.where(end == 0, 1, length - 2)
        return jnp.logical_not(jnp.logical_and(at_end, owner == beside))

    for owner in range(length):

        @pl.when(filled(owner))
        def _():
            for j, m, r in pieces:
                dst = nodes.at[1 - c, owner * owned + j, m, band(r)]
                remote(dst, dst, c_send.at[owner, j, m, r], c_recv.at[owner, j, m, r], twin).wait_recv()

    def products(h, held, fresh):
        for t in range(terms):
            a, b = firsts[t], seconds[t]
            e, f = left_entries[t], right_entries[t]
            k = jnp.where(holds(z, b), b - home, jnp.where(f == slot1, owned + 1, owned))
            parts = complex_mul(nodes[h, e, 0], nodes[h, e, 1], held[k, 0], held[k, 1])
            factor = (wc_ref[t].astype(jnp.float32) - 3.5) * 0.5
            for j in range(owned):
                n = home + j
                count = (a == n).astype(jnp.float32) + (b == n).astype(jnp.float32)
                weight = factor * count
                for m in range(2):
                    if t == 0 and fresh:
                        sums[c, j, m] = weight * parts[m]
                    else:
                        sums[c, j, m] = sums[c, j, m] + weight * parts[m]

    products(x, rows, True)
    for k in range(owned + FOREIGN):
        for m in range(2):
            for r in range(PIECES):
                dst = others.at[k, m, band(r)]
                remote(dst, dst, x_send.at[k, m, r], x_recv.at[k, m, r], across).wait_recv()
    products(1 - x, others, False)

    for j in range(owned):
        for m in range(2):
            s_copy(c, j, m).start()
    for h in (c, 1 - c):
        for j in range(owned):
            if h is not c:
                for m in range(2):
                    s_copy(h, j, m).wait_recv()
            choice = rp_ref[home + j]
            here = [jnp.where(h == x, rows[choice, m], others[choice, m]) for m in range(2)]
            parts = complex_mul(sums[h, j, 0], sums[h, j, 1], here[0], here[1])
            for m in range(2):
                out_ref[m, j] = parts[m] if h is c else out_ref[m, j] + parts[m]

    for j in range(owned):
        for m in range(2):
            s_copy(c, j, m).wait_send()
    for piece in pieces:
        x_copy(*piece, own_at(*piece)).wait_send()
    for s in range(FOREIGN):
        for m in range(2):
            for r in range(PIECES):
                x_copy(owned + s, m, r, rows.at[owned + s, m, band(r)]).wait_send()
    for step in range(length - 1):
        for way in range(2):

            @pl.when(z_sends(way, step))
            def _():
                for piece in pieces:
                    z_copy(way, step, *piece, own_at(*piece)).wait_send()

    for owner in range(length):

        @pl.when(filled(owner))
        def _():
            for piece in pieces:
                c_copy(owner, *piece, own_at(*piece)).wait_send()


def line_body(meson_nodes, term_nodes, weight_codes, resident_pick):
    length = lax.axis_size("node")
    _, owned, height, width = meson_nodes.shape
    terms = term_nodes.shape[0]
    block = (height, width)
    vmem = pl.BlockSpec(memory_space=pltpu.VMEM)
    smem = pl.BlockSpec(memory_space=pltpu.SMEM)
    dma = pltpu.SemaphoreType.DMA
    slots = owned + FOREIGN
    return pl.pallas_call(
        functools.partial(line_kernel, length, owned, terms),
        out_shape=jax.ShapeDtypeStruct(meson_nodes.shape, jnp.float32),
        in_specs=[pl.BlockSpec(memory_space=pl.ANY), smem, smem, smem],
        out_specs=vmem,
        scratch_shapes=[
            pltpu.VMEM((2, length * owned, 2) + block, jnp.float32),
            pltpu.VMEM((slots, 2) + block, jnp.float32),
            pltpu.VMEM((slots, 2) + block, jnp.float32),
            pltpu.VMEM((2, owned, 2) + block, jnp.float32),
            pltpu.VMEM(((length - 2) * owned, 2) + block, jnp.float32),
            dma((2, owned, 2, PIECES)),
            dma((2, length - 1, owned, 2, PIECES)),
            dma((2, length - 1, owned, 2, PIECES)),
            dma((length, owned, 2, PIECES)),
            dma((length, owned, 2, PIECES)),
            dma((slots, 2, PIECES)),
            dma((slots, 2, PIECES)),
            dma((owned, 2)),
            dma((owned, 2)),
        ],
        compiler_params=pltpu.CompilerParams(
            collective_id=0, has_side_effects=True, vmem_limit_bytes=56 << 20
        ),
    )(meson_nodes, term_nodes.T, weight_codes, resident_pick)


def body(meson_nodes, term_nodes, weight_codes, resident_pick):
    length, owned = lax.axis_size("node"), meson_nodes.shape[1]
    square = meson_nodes.shape[2] == meson_nodes.shape[3]
    halves = lax.axis_size("sub") == 2 and lax.axis_size("rep") == 2
    held = 2 * length * meson_nodes.size * 4
    fits = held <= 16 << 20 and term_nodes.shape[0] <= (length - 2) * owned
    if square and halves and fits and owned == FOREIGN and length == 4:
        return line_body(meson_nodes, term_nodes, weight_codes, resident_pick)
    return wide_body(meson_nodes, term_nodes, weight_codes, resident_pick)


def solution(mesh):
    in_specs = (P(None, ("grp", "node"), "sub", "rep"), P("grp", None), P("grp"), P("grp"))
    out_specs = P(None, ("grp", "node"), "sub", "rep")
    return jax.shard_map(body, mesh=mesh, in_specs=in_specs, out_specs=out_specs, check_vma=False)
```

profile of v0, /device:TPU:0, one launch (start us, length us, event | category | flops | bytes accessed | tf_op | source)
XLA Modules:
  0.0 70.3 jit_solution(8281652200350137005)
XLA Ops:
  0.0 68.0 %shard_map.46 = f32[2,2,256,256]{3,2,1,0:T(8,128)} custom-call(f32[2,2,256,256]{3,2,1,0:T(8,128)} %x_ref.1, s32[2,4]{1,0:T(2,128)} %bitcast.1, s32[4]{0:T(128)} %wc_ref.1, s32[8]{0:T(128)} %rp_ref.1), custom_call_target="tpu_custom_call" | custom-call | tf_op jit(solution)/shard_map/pallas_call | solution.py:419
  68.0 2.3 %copy.6 = f32[2,2,256,256]{3,2,1,0:T(8,128)} copy(f32[2,2,256,256]{3,2,1,0:T(8,128)} %shard_map.46) | data formatting | bytes 2097152
where the time goes:
time: 71 us; the launch traced here: 70.3 us
  Pallas kernels  68 us (96%)
  local copies, waits for them, and re-layouts  2.29 us (3%)
    pallas_call x1, Pallas kernels, line_body(): pl.pallas_call(functools.partial(line_kernel, length, owned, terms), out_...  68 us
    unnamed x1, local copies, waits for them, and re-layouts  2.29 us

commit v1 on v0

--- a/solution.py
+++ b/solution.py
@@ -418,7 +418,7 @@
     slots = owned + FOREIGN
     return pl.pallas_call(
         functools.partial(line_kernel, length, owned, terms),
-        out_shape=jax.ShapeDtypeStruct(meson_nodes.shape, jnp.float32),
+        out_shape=pltpu.VMEM(meson_nodes.shape, jnp.float32),
         in_specs=[pl.BlockSpec(memory_space=pl.ANY), smem, smem, smem],
         out_specs=vmem,
         scratch_shapes=[
@@ -438,7 +438,7 @@
             dma((owned, 2)),
         ],
         compiler_params=pltpu.CompilerParams(
-            collective_id=0, has_side_effects=True, vmem_limit_bytes=56 << 20
+            collective_id=0, has_side_effects=True, vmem_limit_bytes=58 << 20
         ),
     )(meson_nodes, term_nodes.T, weight_codes, resident_pick)
 

time: 71 us -> 68.7 us (0.968)
  local copies, waits for them, and re-layouts: 2.29 us -> 0.97 us
  Pallas kernels: 68 us -> 67 us
    unnamed x1, local copies, waits for them, and re-layouts: 2.29 us -> 0.97 us
    pallas_call x1, Pallas kernels: 68 us -> 67 us  [line_body(): pl.pallas_call(functools.partial(line_kernel, length, owned, terms), out_...]
where the time goes in v1:
time: 68.7 us; the launch traced here: 68 us
  Pallas kernels  67 us (98%)
  local copies, waits for them, and re-layouts  0.97 us (1%)
    pallas_call x1, Pallas kernels, line_body(): pl.pallas_call(functools.partial(line_kernel, length, owned, terms), out_...  67 us

profile of v1, /device:TPU:0, one launch (start us, length us, event | category | flops | bytes accessed | tf_op | source)
XLA Modules:
  0.0 68.0 jit_solution(9058050985644393200)
XLA Ops:
  0.0 67.0 %shard_map.46 = f32[2,2,256,256]{3,2,1,0:T(8,128)S(1)} custom-call(f32[2,2,256,256]{3,2,1,0:T(8,128)} %x_ref.1, s32[2,4]{1,0:T(2,128)} %bitcast.1, s32[4]{0:T(128)} %wc_ref.1, s32[8]{0:T(128)} %rp_ref.1), custom_call_target="tpu_custom_call" | custom-call | tf_op jit(solution)/shard_map/pallas_call | solution.py:419
  67.0 1.0 %copy.6 = f32[2,2,256,256]{3,2,1,0:T(8,128)} copy(f32[2,2,256,256]{3,2,1,0:T(8,128)S(1)} %shard_map.46) | data formatting | bytes 2097152

commit v2 on v1

v2 whole, which is shorter than its diff:
```python
import functools

import jax
import jax.numpy as jnp
from jax import lax
from jax.experimental import pallas as pl
from jax.experimental.pallas import tpu as pltpu
from jax.sharding import PartitionSpec as P


def complex_step(full_left, segment):
    highest = lax.Precision.HIGHEST
    real_part = jnp.einsum(
        "kij,kjl->kil",
        full_left[0],
        segment[0],
        precision=highest,
        preferred_element_type=jnp.float32,
    ) - jnp.einsum(
        "kij,kjl->kil",
        full_left[1],
        segment[1],
        precision=highest,
        preferred_element_type=jnp.float32,
    )
    imag_part = jnp.einsum(
        "kij,kjl->kil",
        full_left[0],
        segment[1],
        precision=highest,
        preferred_element_type=jnp.float32,
    ) + jnp.einsum(
        "kij,kjl->kil",
        full_left[1],
        segment[0],
        precision=highest,
        preferred_element_type=jnp.float32,
    )
    return jnp.stack([real_part, imag_part])


def wide_body(meson_nodes, term_nodes, weight_codes, resident_pick):
    node_count = lax.axis_size("node")
    owned = meson_nodes.shape[1]
    row_count = meson_nodes.shape[2]
    col_count = meson_nodes.shape[3]
    band = row_count // node_count
    total_nodes = owned * node_count
    term_count = term_nodes.shape[0]
    banded = meson_nodes.reshape(2, owned, node_count, band * col_count)
    spread = lax.all_to_all(banded, "node", split_axis=2, concat_axis=1, tiled=True).reshape(
        2, total_nodes, band * col_count
    )
    leading = term_nodes[:, 0]
    trailing = term_nodes[:, 1]
    worker_ids = jnp.arange(node_count, dtype=jnp.int32)
    slot_count = term_count // node_count
    table = jnp.arange(slot_count, dtype=jnp.int32)[None, :] * node_count + worker_ids[:, None]
    active = jnp.ones(table.shape, jnp.float32)
    first_table = leading[table]
    second_table = trailing[table]
    factors = active * (weight_codes[table].astype(jnp.float32) - 3.5) * 0.5
    wanted = jnp.stack([first_table.T, second_table.T], axis=1)
    picked = jnp.take(spread, wanted, axis=1)
    fetched = lax.all_to_all(picked, "node", split_axis=3, concat_axis=3, tiled=True).reshape(
        2, slot_count, 2, row_count, col_count
    )
    left_rows = fetched[:, :, 0]
    right_band = fetched[:, :, 1]
    left_full = lax.all_gather(left_rows, "rep", axis=3, tiled=True)
    products = complex_step(left_full, lax.all_gather(right_band, "sub", axis=2, tiled=True))
    outgoing = products.reshape(2, slot_count, node_count, band * col_count)
    returned = lax.all_to_all(outgoing, "node", split_axis=2, concat_axis=1, tiled=True).reshape(
        2, node_count * slot_count, band * col_count
    )
    node_ids = jnp.arange(total_nodes, dtype=jnp.int32)
    incidence = (first_table.reshape(-1)[:, None] == node_ids[None, :]).astype(jnp.float32) + (
        second_table.reshape(-1)[:, None] == node_ids[None, :]
    ).astype(jnp.float32)
    mixing = factors.reshape(-1)[:, None] * incidence
    summed = jnp.einsum("mn,cmx->cnx", mixing, returned, precision=lax.Precision.HIGHEST)
    owner_sum = lax.all_to_all(
        summed.reshape(2, total_nodes, 1, band * col_count),
        "node",
        split_axis=1,
        concat_axis=2,
        tiled=True,
    ).reshape(2, owned, row_count, col_count)
    sum_full = lax.all_gather(owner_sum, "rep", axis=3, tiled=True)
    own_index = lax.axis_index("node")
    picks = lax.dynamic_slice_in_dim(resident_pick, own_index * owned, owned)
    resident = jnp.take(meson_nodes, picks, axis=1)
    return complex_step(sum_full, lax.all_gather(resident, "sub", axis=2, tiled=True))


MESH = pl.DeviceIdType.MESH
UNITS = (2,) * 15 + (1, 1)
LEADS = (4, 3, 3, 2, 2)
BATCHES = (2,) * 6 + (1,) * 5
GROUPS = 4


def split(value):
    high = value.astype(jnp.bfloat16)
    return high, (value - high.astype(jnp.float32)).astype(jnp.bfloat16)


def dot(p, q):
    return jnp.dot(p, q, preferred_element_type=jnp.float32)


def stacked_mul(l0, l1, right):
    rows = l0.shape[0]
    a, b = split(l0)
    c, d = split(l1)
    four = jnp.concatenate([a, b, c, d], axis=0)
    two = jnp.concatenate([a, c], axis=0)
    by_real, by_imag = dot(four, right(0)), dot(four, right(2))
    low_real, low_imag = dot(two, right(1)), dot(two, right(3))

    def part(value, i):
        return value[i * rows : (i + 1) * rows]

    def product(high, low, i):
        return part(high, 2 * i) + (part(high, 2 * i + 1) + part(low, i))

    real = product(by_real, low_real, 0) - product(by_imag, low_imag, 1)
    imag = product(by_imag, low_imag, 0) + product(by_real, low_real, 1)
    return real, imag


def sliced_mul(left, r0, r1):
    def mul(i, value):
        high, low = split(value)
        return dot(left(i), high) + (dot(left(i), low) + dot(left(i + 1), high))

    both, other, cross = mul(0, r0), mul(2, r1), mul(4, r0 + r1)
    return both - other, cross - both - other


def packed_mul(left, r0, r1):
    def mul(i, value):
        high, low = split(value)
        return dot(left(i), jnp.concatenate([high, high, low], axis=0))

    both, other, cross = mul(0, r0), mul(1, r1), mul(2, r0 + r1)
    return both - other, cross - both - other


def pieces_of(height):
    unit = height // sum(UNITS)
    pieces, at = [], 0
    for size in UNITS:
        pieces.append((at, size * unit))
        at += size * unit
    return pieces


def arrivals_of(pieces):
    order, sent = [], 0
    for r in range(len(pieces)):
        lead = LEADS[r] if r < len(LEADS) else 1 + (r >= len(pieces) - 2)
        while sent < min(r + lead, len(pieces)):
            order.append((0, sent))
            sent += 1
        order.append((1, r))
    return order


def plan_of(order, pieces, height):
    after = {
        (0, 1): [("pass", 1), ("right", 0), ("right", 1), ("right", 2), ("right", 3), ("left", 0)],
        (0, 2): [("pass", 3), ("left", 1)],
        (1, 0): [("pass", 5), ("facing", 0)],
        (0, 4): [("pass", 7)],
        (1, 3): [("pass", 9), ("facing", 1)],
        (1, 4): [("pass", 11)],
        (1, 5): [("facing", 2)],
        (0, 6): [("pass", 13)],
        (1, 7): [("facing", 3), ("turn", 0)],
        (0, 8): [("pass", 16), ("turn", 1), ("turn", 2)],
        (1, 8): [("turn", 3), ("up", 0)],
        (0, 9): [("up", 1)],
        (1, 9): [("down", 0)],
        (0, 10): [("turn", 4), ("down", 1)],
        (1, 10): [("mine", 0)],
        (0, 12): [("turn", 5), ("up", 2)],
        (0, 13): [("turn", 6), ("down", 2)],
        (1, 13): [("theirs", 0)],
        (0, 14): [("turn", 7), ("mine", 1)],
        (1, 14): [("up", 3)],
        (0, 16): [("turn", 8)],
        (1, 15): [("theirs", 1)],
        (1, 16): [("turn", 9), ("turn", 10), ("up", 4), ("down", 3), ("mine", 2), ("down", 4), ("theirs", 2)],
    }
    plan = []
    for kind, r in order:
        plan.append(("far" if kind else "near", r))
        plan += after.get((kind, r), [])
    return plan


def line_kernel(
    length, owned, terms,
    x_ref, tn_ref, wc_ref, rp_ref, out_ref,
    own, beside, facing, outer, inner, far, near_pick, far_pick,
    mixes, turned, turned_far, lefts, packs, rights, ups,
    loc_sem, z_send, z_recv, o_recv, x_send, x_recv, t_recv, c_send, c_recv, m_recv, u_recv, ready,
):
    z = lax.axis_index("node")
    x = lax.axis_index("sub")
    c = lax.axis_index("rep")
    g = lax.axis_index("grp")
    above = (g, z + 1, x, c)
    below = (g, z - 1, x, c)
    across = (g, z, 1 - x, c)
    twin = (g, z, x, 1 - c)
    height = x_ref.shape[2]
    pieces = pieces_of(height)
    count = len(pieces)
    order = arrivals_of(pieces)
    group = height // GROUPS
    groups = [(at, group) for at in range(0, height, group)]
    slices = [(0, 2 * group), (2 * group, group), (3 * group, group)]
    lifts = groups[:3] + [(3 * group, group // 2), (3 * group + group // 2, group // 2)]
    batches, first = [], 0
    for size in BATCHES:
        batches.append((pieces[first][0], sum(tall for _, tall in pieces[first : first + size])))
        first += size
    closing = {sum(BATCHES[: k + 1]) - 1: k for k in range(len(BATCHES))}
    raws = [(at, group // 2) for at in range(0, height, group // 2)]
    low = z < length // 2
    is_end = jnp.logical_or(z == 0, z == length - 1)
    is_mid = jnp.logical_not(is_end)
    end = jnp.where(low, 0, length - 1)
    far_end = length - 1 - end
    toward_end = (g, jnp.where(low, z - 1, z + 1), x, c)
    toward_mid = (g, jnp.where(low, z + 1, z - 1), x, c)

    def remote(src, dst, send, recv, device):
        return pltpu.make_async_remote_copy(
            src_ref=src, dst_ref=dst, send_sem=send, recv_sem=recv, device_id=device, device_id_type=MESH
        )

    def rows(r):
        return pl.ds(*pieces[r])

    def raw_copy(k):
        span = pl.ds(*raws[k])
        return remote(
            x_ref.at[:, :, span], outer.at[:, :, span], z_send.at[0], o_recv.at[k], toward_mid
        )

    def own_copy(r):
        return remote(
            x_ref.at[:, :, rows(r)], inner.at[:, :, rows(r)], z_send.at[1], z_recv.at[0, r], toward_mid
        )

    def pass_copy(r):
        return remote(
            outer.at[:, :, rows(r)], far.at[:, :, rows(r)], z_send.at[2], z_recv.at[1, r], toward_mid
        )

    def near_copy(r):
        return remote(
            near_pick.at[:, :, rows(r)], inner.at[:, :, rows(r)], z_send.at[3], z_recv.at[0, r], toward_end
        )

    def far_copy(r):
        return remote(
            far_pick.at[:, :, rows(r)], far.at[:, :, rows(r)], z_send.at[4], z_recv.at[1, r], toward_end
        )

    def x_copy(k):
        span = pl.ds(*groups[k])
        return remote(
            x_ref.at[:, :, span], facing.at[:, :, span], x_send.at[0], x_recv.at[k], across
        )

    def turned_copy(k):
        span = pl.ds(*batches[k])
        return remote(
            turned.at[:, :, span], turned_far.at[:, :, span], x_send.at[1], t_recv.at[k], across
        )

    def c_copy(j):
        return remote(x_ref.at[:, j], beside.at[:, j], c_send.at[0], c_recv.at[j], twin)

    def mix_copy(slot, k):
        part = mixes.at[slot, :, :, pl.ds(*batches[k])]
        return remote(part, part, c_send.at[1], m_recv.at[k], twin)

    def up_copy(slot, k):
        part = ups.at[slot, :, :, pl.ds(*lifts[k])]
        return remote(part, part, c_send.at[2], u_recv.at[k], twin)

    barrier = pltpu.get_barrier_semaphore()
    ENTER = ((z < length - 1, above, z > 0, below), (x == 0, across, x == 1, across), (c == 1, twin, c == 0, twin))
    waits = 0
    for early, later_device, late, _ in ENTER:

        @pl.when(early)
        def _():
            pl.semaphore_signal(barrier, inc=1, device_id=later_device, device_id_type=MESH)

        waits = waits + late.astype(jnp.int32)

    @pl.when(waits > 0)
    def _():
        pl.semaphore_wait(barrier, waits)

    for i, (_, _, late, early_device) in enumerate(ENTER):

        @pl.when(late)
        def _():
            pl.semaphore_signal(ready.at[i], inc=1, device_id=early_device, device_id_type=MESH)

    def meet(i):
        @pl.when(ENTER[i][0])
        def _():
            pl.semaphore_wait(ready.at[i], 1)

    first_own = order[: order.index((1, 0))]
    passing = {"sent": len(first_own), "raw": 0}

    def send_until(r):
        last = order.index((1, r)) + 1

        @pl.when(is_mid)
        def _():
            for kind, p in order[passing["sent"] : last]:
                if kind == 0:
                    own_copy(p).start()
                else:
                    while raws[passing["raw"] - 1][0] + raws[0][1] < sum(pieces[p]) or passing["raw"] == 0:
                        raw_copy(passing["raw"]).wait_recv()
                        passing["raw"] += 1
                    pass_copy(p).start()

        passing["sent"] = last

    def open_sends():
        @pl.when(is_end)
        def _():
            for k in range(len(raws)):
                raw_copy(k).start()

        @pl.when(is_mid)
        def _():
            for _, p in first_own:
                own_copy(p).start()

    @pl.when(jnp.logical_not(low))
    def _():
        open_sends()

    meet(0)

    @pl.when(low)
    def _():
        open_sends()

    meet(2)
    for j in range(owned):
        c_copy(j).start()
    local = pltpu.make_async_copy(x_ref, own, loc_sem.at[0])
    local.start()
    meet(1)
    for k in range(GROUPS):
        x_copy(k).start()

    firsts = [tn_ref[0, t] for t in range(terms)]
    seconds = [tn_ref[1, t] for t in range(terms)]
    factors = [(wc_ref[t].astype(jnp.float32) - 3.5) * 0.5 for t in range(terms)]
    choices = [rp_ref[z * owned + n] for n in range(owned)]
    spots = (length - 2) * owned

    def holds(owner, n):
        return jnp.logical_and(n >= owner * owned, n < owner * owned + owned)

    def rank_of(n):
        owner = n // owned
        return jnp.where(end == 0, owner, length - 1 - owner) * owned + n - owner * owned

    def node_of(rank):
        far_owner = rank // owned
        return jnp.where(end == 0, far_owner, length - 1 - far_owner) * owned + rank % owned

    def partner_ranks():
        ranks = []
        for a, b in zip(firsts, seconds):
            here, there = holds(end, a), holds(end, b)
            rank = jnp.where(here, rank_of(b), rank_of(a))
            ranks.append(jnp.where(here != there, rank, owned))
        below_rank, found = length * owned, []
        for _ in range(spots):
            best = owned
            for rank in ranks:
                best = jnp.where(jnp.logical_and(rank < below_rank, rank > best), rank, best)
            found.append(best)
            below_rank = best
        return found[::-1]

    wanted = partner_ranks()
    spot_nodes = []
    for i in range(spots):
        node = node_of(wanted[i])
        if i < spots - 1:
            node = jnp.where(wanted[i] == wanted[i + 1], -1, node)
        spot_nodes.append(node)
    home = z * owned
    near_mid = jnp.where(low, z + 1, z - 1) * owned
    entry_nodes = [home + j for j in range(owned)]
    entry_nodes += [jnp.where(is_mid, near_mid + j, spot_nodes[j]) for j in range(owned)]
    entry_nodes += [jnp.where(is_mid, far_end * owned + j, spot_nodes[owned + j]) for j in range(owned)]
    entry_nodes += [end * owned + j for j in range(owned)]
    zero = jnp.float32(0)

    def weight_of(keys, partners, n, node):
        total = zero
        for t in range(terms):
            match = jnp.logical_and(keys[t] == n, partners[t] == node)
            total = total + jnp.where(match, factors[t], zero)
        return total

    weights = [
        [weight_of(keys, partners, home + n, node) for node in entry_nodes]
        for keys, partners in ((seconds, firsts), (firsts, seconds))
        for n in range(owned)
    ]

    def blend(r, whole):
        for m in range(2):
            held = [ref[m, j, rows(r)] for ref in (own, inner, far) for j in range(owned)]
            if whole:
                held += [outer[m, j, rows(r)] for j in range(owned)]
            for q, row in enumerate(weights):
                total = row[0] * held[0]
                for value, part in zip(row[1:], held[1:]):
                    total = total + value * part
                mixes[c, q, m, rows(r)] = total

    def pick(dst, i, spot, r, sources):
        for m in range(2):
            chosen = sources[0][0][m, sources[0][1], rows(r)]
            for k, (ref, j) in enumerate(sources[1:]):
                chosen = jnp.where(wanted[spot] == owned + 1 + k, ref[m, j, rows(r)], chosen)
            dst[m, i, rows(r)] = chosen

    ranked = [(ref, j) for ref in (own, inner, far) for j in range(owned)]

    def arrive(kind, r):
        @pl.when(is_mid)
        def _():
            if kind == 0:
                own_copy(r).wait_recv()
                for i in range(owned):
                    pick(near_pick, i, i, r, ranked[: owned + 1 + i])
                near_copy(r).start()
            else:
                pass_copy(r).wait_recv()
                for i in range(owned):
                    pick(far_pick, i, owned + i, r, ranked[: 2 * owned + 1 + i])
                far_copy(r).start()
                blend(r, True)

        @pl.when(is_end)
        def _():
            if kind == 0:
                near_copy(r).wait_recv()
            else:
                far_copy(r).wait_recv()
                blend(r, False)

        if kind == 1 and r in closing:
            mix_copy(c, closing[r]).start()

    def clear():
        out_ref[...] = jnp.zeros_like(out_ref)

    def put_right(ref, h, k):
        span = pl.ds(*groups[k])
        for j in range(owned):
            for m in range(2):
                for i, part in enumerate(split(ref[m, j, span])):
                    rights[j, 2 * m + i, h, span] = part

    def put_left(ref, h, n):
        re, im = ref[0, n], ref[1, n]
        for k, value in enumerate((re, im, re + im)):
            high, low_part = split(value)
            at, size = slices[0]
            lefts[n, 2 * k, h] = high[:, at : at + size]
            lefts[n, 2 * k + 1, h] = low_part[:, at : at + size]
            for i, (at, size) in enumerate(slices[1:]):
                part = high[:, at : at + size]
                packs[n, k, h, i] = jnp.concatenate([part, low_part[:, at : at + size], part], axis=1)

    def prepare_facing(k):
        x_copy(k).wait_recv()
        put_right(facing, 1 - x, k)

    def prepare_left(n):
        put_left(own, c, n)
        c_copy(n).wait_recv()
        put_left(beside, 1 - c, n)

    def right_of(n):
        return lambda i: rights[n, i].reshape(2 * height, height)

    def wide(ref, q, m, span):
        return jnp.concatenate([ref[h, q, m, span] for h in range(2)], axis=1)

    def turn(k):
        mix_copy(1 - c, k).wait_recv()
        span = pl.ds(*batches[k])
        for n in range(owned):
            q = owned + n
            parts = stacked_mul(wide(mixes, q, 0, span), wide(mixes, q, 1, span), right_of(choices[n]))
            for m in range(2):
                turned[n, m, span] = parts[m]
        turned_copy(k).start()

    def raise_up(k):
        span = pl.ds(*lifts[k])
        for n in range(owned):
            parts = stacked_mul(wide(mixes, n, 0, span), wide(mixes, n, 1, span), right_of(n))
            for m in range(2):
                ups[c, n, m, span] = parts[m]
        up_copy(c, k).start()

    def finish_up(k):
        up_copy(1 - c, k).wait_recv()
        span = pl.ds(*lifts[k])
        for n in range(owned):
            parts = stacked_mul(wide(ups, n, 0, span), wide(ups, n, 1, span), right_of(choices[n]))
            for m in range(2):
                out_ref[m, n, span] = out_ref[m, n, span] + parts[m]

    def add_slice(ref, h, k):
        at, size = slices[k]
        for n in range(owned):
            r0, r1 = ref[n, 0, at : at + size], ref[n, 1, at : at + size]
            if k == 0:
                parts = sliced_mul(lambda i: lefts[n, i, h], r0, r1)
            else:
                parts = packed_mul(lambda i: packs[n, i, h, k - 1], r0, r1)
            for m in range(2):
                out_ref[m, n] = out_ref[m, n] + parts[m]

    def add_theirs(k):
        at, size = slices[k]
        for i, (start, _) in enumerate(batches):
            if at <= start < at + size:
                turned_copy(i).wait_recv()
        add_slice(turned_far, 1 - x, k)

    clear()
    local.wait()

    plan = plan_of(order, pieces, height)
    actions = {
        "pass": send_until,
        "near": lambda r: arrive(0, r),
        "far": lambda r: arrive(1, r),
        "right": lambda k: put_right(own, x, k),
        "left": prepare_left,
        "facing": prepare_facing,
        "turn": turn,
        "up": raise_up,
        "down": finish_up,
        "mine": lambda k: add_slice(turned, x, k),
        "theirs": add_theirs,
    }
    for name, i in plan:
        with jax.named_scope(f"{name}{i}"):
            actions[name](i)

    remote(x_ref, facing, x_send.at[0], x_recv.at[0], across).wait_send()
    remote(turned, turned_far, x_send.at[1], t_recv.at[0], across).wait_send()
    remote(x_ref, beside, c_send.at[0], c_recv.at[0], twin).wait_send()
    remote(mixes.at[c], mixes.at[c], c_send.at[1], m_recv.at[0], twin).wait_send()
    remote(ups.at[c], ups.at[c], c_send.at[2], u_recv.at[0], twin).wait_send()

    @pl.when(is_end)
    def _():
        remote(x_ref, outer, z_send.at[0], o_recv.at[0], toward_mid).wait_send()

    @pl.when(is_mid)
    def _():
        remote(x_ref, inner, z_send.at[1], z_recv.at[0, 0], toward_mid).wait_send()
        remote(outer, far, z_send.at[2], z_recv.at[1, 0], toward_mid).wait_send()
        remote(near_pick, inner, z_send.at[3], z_recv.at[0, 0], toward_end).wait_send()
        remote(far_pick, far, z_send.at[4], z_recv.at[1, 0], toward_end).wait_send()


def line_body(meson_nodes, term_nodes, weight_codes, resident_pick):
    length = lax.axis_size("node")
    _, owned, height, width = meson_nodes.shape
    terms = term_nodes.shape[0]
    block = (height, width)
    vmem = pl.BlockSpec(memory_space=pltpu.VMEM)
    smem = pl.BlockSpec(memory_space=pltpu.SMEM)
    dma = pltpu.SemaphoreType.DMA
    count = len(UNITS)
    whole = pltpu.VMEM((2, owned) + block, jnp.float32)
    return pl.pallas_call(
        functools.partial(line_kernel, length, owned, terms),
        out_shape=pltpu.VMEM(meson_nodes.shape, jnp.float32),
        in_specs=[pl.BlockSpec(memory_space=pl.ANY), smem, smem, smem],
        out_specs=vmem,
        scratch_shapes=[whole] * 8
        + [
            pltpu.VMEM((2, 2 * owned, 2) + block, jnp.float32),
            pltpu.VMEM((owned, 2) + block, jnp.float32),
            pltpu.VMEM((owned, 2) + block, jnp.float32),
            pltpu.VMEM((owned, 6, 2, height, width // 2), jnp.bfloat16),
            pltpu.VMEM((owned, 3, 2, 2, height, 3 * width // GROUPS), jnp.bfloat16),
            pltpu.VMEM((owned, 4, 2) + block, jnp.bfloat16),
            pltpu.VMEM((2, owned, 2) + block, jnp.float32),
            dma((1,)),
            dma((5,)),
            dma((2, count)),
            dma((2 * GROUPS,)),
            dma((2,)),
            dma((GROUPS,)),
            dma((len(BATCHES),)),
            dma((3,)),
            dma((owned,)),
            dma((len(BATCHES),)),
            dma((GROUPS + 1,)),
            pltpu.SemaphoreType.REGULAR((3,)),
        ],
        compiler_params=pltpu.CompilerParams(
            collective_id=0, has_side_effects=True, vmem_limit_bytes=58 << 20
        ),
    )(meson_nodes, term_nodes.T, weight_codes, resident_pick)


def body(meson_nodes, term_nodes, weight_codes, resident_pick):
    length, owned = lax.axis_size("node"), meson_nodes.shape[1]
    height = meson_nodes.shape[2]
    square = height == meson_nodes.shape[3]
    halves = lax.axis_size("sub") == 2 and lax.axis_size("rep") == 2
    fits = height % (8 * sum(UNITS)) == 0 and term_nodes.shape[0] <= (length - 2) * owned
    if square and halves and fits and owned == 2 and length == 4:
        return line_body(meson_nodes, term_nodes, weight_codes, resident_pick)
    return wide_body(meson_nodes, term_nodes, weight_codes, resident_pick)


def solution(mesh):
    in_specs = (P(None, ("grp", "node"), "sub", "rep"), P("grp", None), P("grp"), P("grp"))
    out_specs = P(None, ("grp", "node"), "sub", "rep")
    return jax.shard_map(body, mesh=mesh, in_specs=in_specs, out_specs=out_specs, check_vma=False)
```

time: 68.7 us -> 63.2 us (0.920)
  Pallas kernels: 67 us -> 62.1 us
    pallas_call x1, Pallas kernels: 67 us -> 62.1 us  [line_body(): pl.pallas_call(functools.partial(line_kernel, length, owned, terms), out_...]
where the time goes in v2:
time: 63.2 us; the launch traced here: 63.1 us
  Pallas kernels  62.1 us (98%)
  local copies, waits for them, and re-layouts  0.97 us (2%)
    pallas_call x1, Pallas kernels, line_body(): pl.pallas_call(functools.partial(line_kernel, length, owned, terms), out_...  62.1 us

profile of v2, /device:TPU:0, one launch (start us, length us, event | category | flops | bytes accessed | tf_op | source)
XLA Modules:
  0.0 63.1 jit_solution(7030168204829107928)
XLA Ops:
  0.0 62.1 %shard_map.46 = f32[2,2,256,256]{3,2,1,0:T(8,128)S(1)} custom-call(f32[2,2,256,256]{3,2,1,0:T(8,128)} %x_ref.1, s32[2,4]{1,0:T(2,128)} %bitcast.1, s32[4]{0:T(128)} %wc_ref.1, s32[8]{0:T(128)} %rp_ref.1), custom_call_target="tpu_custom_call" | custom-call | tf_op jit(solution)/shard_map/pallas_call | solution.py:607
  62.1 1.0 %copy.6 = f32[2,2,256,256]{3,2,1,0:T(8,128)} copy(f32[2,2,256,256]{3,2,1,0:T(8,128)S(1)} %shard_map.46) | data formatting | bytes 2097152

commit v3 on v2

--- a/solution.py
+++ b/solution.py
@@ -94,10 +94,11 @@
 
 
 MESH = pl.DeviceIdType.MESH
-UNITS = (2,) * 15 + (1, 1)
+UNITS = (2,) * 14 + (1, 1, 1, 1)
 LEADS = (4, 3, 3, 2, 2)
-BATCHES = (2,) * 6 + (1,) * 5
+BATCHES = (2,) * 6 + (1,) * 6
 GROUPS = 4
+TAIL = (14, 15, 16, 17)
 
 
 def split(value):
@@ -129,6 +130,15 @@
     return real, imag
 
 
+def plain_mul(l0, l1, right):
+    def mul(value, i):
+        high, low = split(value)
+        return dot(high, right(i)) + (dot(high, right(i + 1)) + dot(low, right(i)))
+
+    both, other, cross = mul(l0, 0), mul(l1, 2), mul(l0 + l1, 4)
+    return both - other, cross - both - other
+
+
 def sliced_mul(left, r0, r1):
     def mul(i, value):
         high, low = split(value)
@@ -159,7 +169,7 @@
 def arrivals_of(pieces):
     order, sent = [], 0
     for r in range(len(pieces)):
-        lead = LEADS[r] if r < len(LEADS) else 1 + (r >= len(pieces) - 2)
+        lead = LEADS[r] if r < len(LEADS) else 1
         while sent < min(r + lead, len(pieces)):
             order.append((0, sent))
             sent += 1
@@ -175,23 +185,28 @@
         (0, 4): [("pass", 7)],
         (1, 3): [("pass", 9), ("facing", 1)],
         (1, 4): [("pass", 11)],
-        (1, 5): [("facing", 2)],
+        (1, 5): [("facing", 2), ("end facing", 3), ("end turn", 0), ("end turn", 1)],
         (0, 6): [("pass", 13)],
-        (1, 7): [("facing", 3), ("turn", 0)],
-        (0, 8): [("pass", 16), ("turn", 1), ("turn", 2)],
-        (1, 8): [("turn", 3), ("up", 0)],
-        (0, 9): [("up", 1)],
-        (1, 9): [("down", 0)],
-        (0, 10): [("turn", 4), ("down", 1)],
+        (1, 6): [("end turn", 2)],
+        (1, 7): [("mid facing", 3), ("mid turn", 0)],
+        (0, 8): [("pass", 17), ("mid turn", 1), ("mid turn", 2)],
+        (1, 8): [("turn", 3), ("square", 0)],
+        (0, 9): [("square", 1)],
+        (1, 9): [("square", 2)],
+        (0, 10): [("turn", 4), ("square", 3)],
         (1, 10): [("mine", 0)],
-        (0, 12): [("turn", 5), ("up", 2)],
-        (0, 13): [("turn", 6), ("down", 2)],
+        (0, 11): [("up", 0)],
+        (1, 11): [("up", 1)],
+        (0, 12): [("turn", 5)],
+        (1, 12): [("up", 2)],
+        (0, 13): [("turn", 6)],
         (1, 13): [("theirs", 0)],
-        (0, 14): [("turn", 7), ("mine", 1)],
+        (0, 14): [("turn", 7)],
         (1, 14): [("up", 3)],
-        (0, 16): [("turn", 8)],
-        (1, 15): [("theirs", 1)],
-        (1, 16): [("turn", 9), ("turn", 10), ("up", 4), ("down", 3), ("mine", 2), ("down", 4), ("theirs", 2)],
+        (0, 15): [("mine", 1)],
+        (1, 15): [("turn", 8)],
+        (1, 16): [("turn", 9)],
+        (1, 17): [("turn", 10), ("turn", 11), ("late", 0), ("theirs", 1), ("mine", 2), ("up", 4), ("theirs", 2)],
     }
     plan = []
     for kind, r in order:
@@ -202,10 +217,10 @@
 
 def line_kernel(
     length, owned, terms,
-    x_ref, tn_ref, wc_ref, rp_ref, out_ref,
-    own, beside, facing, outer, inner, far, near_pick, far_pick,
-    mixes, turned, turned_far, lefts, packs, rights, ups,
-    loc_sem, z_send, z_recv, o_recv, x_send, x_recv, t_recv, c_send, c_recv, m_recv, u_recv, ready,
+    x_ref, tn_any, wc_any, rp_any, out_ref,
+    tn_ref, wc_ref, rp_ref, held, faced, outer, inner, far, near_pick, far_pick,
+    mixes, turned, turned_far, lefts, packs, rights, squares,
+    loc_sem, z_send, z_recv, o_recv, x_send, x_recv, t_recv, c_send, c_recv, m_recv, ready,
 ):
     z = lax.axis_index("node")
     x = lax.axis_index("sub")
@@ -215,6 +230,7 @@
     below = (g, z - 1, x, c)
     across = (g, z, 1 - x, c)
     twin = (g, z, x, 1 - c)
+    own, facing = held.at[c], faced.at[c]
     height = x_ref.shape[2]
     pieces = pieces_of(height)
     count = len(pieces)
@@ -228,7 +244,7 @@
         batches.append((pieces[first][0], sum(tall for _, tall in pieces[first : first + size])))
         first += size
     closing = {sum(BATCHES[: k + 1]) - 1: k for k in range(len(BATCHES))}
-    raws = [(at, group // 2) for at in range(0, height, group // 2)]
+    raws = [(0, group // 2), (group // 2, group // 2)] + groups[1:]
     low = z < length // 2
     is_end = jnp.logical_or(z == 0, z == length - 1)
     is_mid = jnp.logical_not(is_end)
@@ -280,20 +296,35 @@
     def turned_copy(k):
         span = pl.ds(*batches[k])
         return remote(
-            turned.at[:, :, span], turned_far.at[:, :, span], x_send.at[1], t_recv.at[k], across
+            turned.at[:, :, span], turned_far.at[:, :, span], x_send.at[1], t_recv.at[slice_of(k)], across
         )
 
-    def c_copy(j):
-        return remote(x_ref.at[:, j], beside.at[:, j], c_send.at[0], c_recv.at[j], twin)
+    def slice_of(k):
+        return max(i for i, (at, _) in enumerate(slices) if at <= batches[k][0])
+
+    def c_copy(slot):
+        return remote(x_ref, held.at[slot], c_send.at[0], c_recv.at[0], twin)
+
+    def face_copy(slot, span):
+        part = faced.at[slot, :, :, span]
+        return remote(part, part, c_send.at[2], c_recv.at[1], twin)
+
+    tail_span = pl.ds(pieces[TAIL[0]][0], sum(pieces[r][1] for r in TAIL))
 
     def mix_copy(slot, k):
-        part = mixes.at[slot, :, :, pl.ds(*batches[k])]
+        span = pl.ds(*batches[k])
+        tail = batches[k][0] >= pieces[TAIL[0]][0]
+        part = mixes.at[slot, pl.ds(owned, owned), :, span] if tail else mixes.at[slot, :, :, span]
         return remote(part, part, c_send.at[1], m_recv.at[k], twin)
 
-    def up_copy(slot, k):
-        part = ups.at[slot, :, :, pl.ds(*lifts[k])]
-        return remote(part, part, c_send.at[2], u_recv.at[k], twin)
-
+    def late_copy(slot):
+        part = mixes.at[slot, pl.ds(0, owned), :, tail_span]
+        return remote(part, part, c_send.at[1], m_recv.at[len(batches)], twin)
+
+    tables = [
+        pltpu.make_async_copy(src, dst, loc_sem.at[1 + i])
+        for i, (src, dst) in enumerate(((tn_any, tn_ref), (wc_any, wc_ref), (rp_any, rp_ref)))
+    ]
     barrier = pltpu.get_barrier_semaphore()
     ENTER = ((z < length - 1, above, z > 0, below), (x == 0, across, x == 1, across), (c == 1, twin, c == 0, twin))
     waits = 0
@@ -332,7 +363,7 @@
                 if kind == 0:
                     own_copy(p).start()
                 else:
-                    while raws[passing["raw"] - 1][0] + raws[0][1] < sum(pieces[p]) or passing["raw"] == 0:
+                    while passing["raw"] == 0 or sum(raws[passing["raw"] - 1]) < sum(pieces[p]):
                         raw_copy(passing["raw"]).wait_recv()
                         passing["raw"] += 1
                     pass_copy(p).start()
@@ -361,14 +392,17 @@
         open_sends()
 
     meet(2)
-    for j in range(owned):
-        c_copy(j).start()
+    c_copy(c).start()
     local = pltpu.make_async_copy(x_ref, own, loc_sem.at[0])
     local.start()
+    for table in tables:
+        table.start()
     meet(1)
     for k in range(GROUPS):
         x_copy(k).start()
 
+    for table in tables:
+        table.wait()
     firsts = [tn_ref[0, t] for t in range(terms)]
     seconds = [tn_ref[1, t] for t in range(terms)]
     factors = [(wc_ref[t].astype(jnp.float32) - 3.5) * 0.5 for t in range(terms)]
@@ -423,22 +457,32 @@
             total = total + jnp.where(match, factors[t], zero)
         return total
 
-    weights = [
-        [weight_of(keys, partners, home + n, node) for node in entry_nodes]
-        for keys, partners in ((seconds, firsts), (firsts, seconds))
-        for n in range(owned)
-    ]
-
-    def blend(r, whole):
+    def weights_for(base):
+        return [
+            [weight_of(keys, partners, base + n, node) for node in entry_nodes]
+            for keys, partners in ((seconds, firsts), (firsts, seconds))
+            for n in range(owned)
+        ]
+
+    weights, end_weights = weights_for(home), weights_for(end * owned)
+
+    def weighted(row, parts):
+        total = row[0] * parts[0]
+        for value, part in zip(row[1:], parts[1:]):
+            total = total + value * part
+        return total
+
+    def blend(r, whole, tail=False):
         for m in range(2):
-            held = [ref[m, j, rows(r)] for ref in (own, inner, far) for j in range(owned)]
+            parts = [ref[m, j, rows(r)] for ref in (own, inner, far) for j in range(owned)]
             if whole:
-                held += [outer[m, j, rows(r)] for j in range(owned)]
+                parts += [outer[m, j, rows(r)] for j in range(owned)]
             for q, row in enumerate(weights):
-                total = row[0] * held[0]
-                for value, part in zip(row[1:], held[1:]):
-                    total = total + value * part
-                mixes[c, q, m, rows(r)] = total
+                mixes[c, q, m, rows(r)] = weighted(row, parts)
+            if tail:
+                for q, row in enumerate(end_weights):
+                    dst = far_pick if q < owned else near_pick
+                    dst[m, q % owned, rows(r)] = weighted(row, parts)
 
     def pick(dst, i, spot, r, sources):
         for m in range(2):
@@ -450,6 +494,9 @@
     ranked = [(ref, j) for ref in (own, inner, far) for j in range(owned)]
 
     def arrive(kind, r):
+        if r in TAIL:
+            return arrive_tail(kind, r)
+
         @pl.when(is_mid)
         def _():
             if kind == 0:
@@ -475,15 +522,52 @@
         if kind == 1 and r in closing:
             mix_copy(c, closing[r]).start()
 
+    def arrive_tail(kind, r):
+        @pl.when(is_mid)
+        def _():
+            if kind == 0:
+                own_copy(r).wait_recv()
+            else:
+                pass_copy(r).wait_recv()
+                blend(r, True, True)
+                near_copy(r).start()
+                if r > TAIL[0]:
+                    far_copy(r - 1).start()
+                if r == TAIL[-1]:
+                    far_copy(r).start()
+
+        if kind == 1:
+
+            @pl.when(is_end)
+            def _():
+                near_copy(r).wait_recv()
+                for n in range(owned):
+                    for m in range(2):
+                        mixes[c, owned + n, m, rows(r)] = inner[m, n, rows(r)]
+
+            mix_copy(c, closing[r]).start()
+
+    def late(_):
+        @pl.when(is_end)
+        def _():
+            for r in TAIL:
+                far_copy(r).wait_recv()
+                for n in range(owned):
+                    for m in range(2):
+                        mixes[c, n, m, rows(r)] = far[m, n, rows(r)]
+
+        late_copy(c).start()
+
     def clear():
         out_ref[...] = jnp.zeros_like(out_ref)
 
     def put_right(ref, h, k):
         span = pl.ds(*groups[k])
         for j in range(owned):
-            for m in range(2):
-                for i, part in enumerate(split(ref[m, j, span])):
-                    rights[j, 2 * m + i, h, span] = part
+            re, im = ref[0, j, span], ref[1, j, span]
+            for k, value in enumerate((re, im, re + im)):
+                for i, part in enumerate(split(value)):
+                    rights[j, 2 * k + i, h, span] = part
 
     def put_left(ref, h, n):
         re, im = ref[0, n], ref[1, n]
@@ -498,12 +582,14 @@
 
     def prepare_facing(k):
         x_copy(k).wait_recv()
+        face_copy(c, pl.ds(*groups[k])).start()
         put_right(facing, 1 - x, k)
 
     def prepare_left(n):
         put_left(own, c, n)
-        c_copy(n).wait_recv()
-        put_left(beside, 1 - c, n)
+        if n == 0:
+            c_copy(1 - c).wait_recv()
+        put_left(held.at[1 - c], 1 - c, n)
 
     def right_of(n):
         return lambda i: rights[n, i].reshape(2 * height, height)
@@ -521,19 +607,24 @@
                 turned[n, m, span] = parts[m]
         turned_copy(k).start()
 
+    def square(i):
+        n, away = i % owned, i // owned
+        ref, h = (faced, 1 - x) if away else (held, x)
+        if i == owned:
+            face_copy(1 - c, pl.ds(0, height)).wait_recv()
+        left = [jnp.concatenate([ref[h2, m, n] for h2 in range(2)], axis=1) for m in range(2)]
+        parts = plain_mul(left[0], left[1], right_of(choices[n]))
+        for m in range(2):
+            for k, part in enumerate(split(parts[m])):
+                squares[n, 2 * m + k, h] = part
+
     def raise_up(k):
         span = pl.ds(*lifts[k])
+        if k == len(lifts) - 1:
+            late_copy(1 - c).wait_recv()
         for n in range(owned):
-            parts = stacked_mul(wide(mixes, n, 0, span), wide(mixes, n, 1, span), right_of(n))
-            for m in range(2):
-                ups[c, n, m, span] = parts[m]
-        up_copy(c, k).start()
-
-    def finish_up(k):
-        up_copy(1 - c, k).wait_recv()
-        span = pl.ds(*lifts[k])
-        for n in range(owned):
-            parts = stacked_mul(wide(ups, n, 0, span), wide(ups, n, 1, span), right_of(choices[n]))
+            right = lambda i: squares[n, i].reshape(2 * height, height)
+            parts = stacked_mul(wide(mixes, n, 0, span), wide(mixes, n, 1, span), right)
             for m in range(2):
                 out_ref[m, n, span] = out_ref[m, n, span] + parts[m]
 
@@ -550,9 +641,10 @@
 
     def add_theirs(k):
         at, size = slices[k]
-        for i, (start, _) in enumerate(batches):
-            if at <= start < at + size:
-                turned_copy(i).wait_recv()
+        span = pl.ds(at, size)
+        remote(
+            turned.at[:, :, span], turned_far.at[:, :, span], x_send.at[1], t_recv.at[k], across
+        ).wait_recv()
         add_slice(turned_far, 1 - x, k)
 
     clear()
@@ -563,24 +655,29 @@
         "pass": send_until,
         "near": lambda r: arrive(0, r),
         "far": lambda r: arrive(1, r),
+        "late": late,
         "right": lambda k: put_right(own, x, k),
         "left": prepare_left,
         "facing": prepare_facing,
         "turn": turn,
         "up": raise_up,
-        "down": finish_up,
+        "square": square,
         "mine": lambda k: add_slice(turned, x, k),
         "theirs": add_theirs,
     }
     for name, i in plan:
-        with jax.named_scope(f"{name}{i}"):
-            actions[name](i)
+        with jax.named_scope(f"{name}{i}".replace(" ", "_")):
+            where, _, what = name.rpartition(" ")
+            if where:
+                pl.when(is_end if where == "end" else is_mid)(functools.partial(actions[what], i))
+            else:
+                actions[what](i)
 
     remote(x_ref, facing, x_send.at[0], x_recv.at[0], across).wait_send()
     remote(turned, turned_far, x_send.at[1], t_recv.at[0], across).wait_send()
-    remote(x_ref, beside, c_send.at[0], c_recv.at[0], twin).wait_send()
+    c_copy(c).wait_send()
     remote(mixes.at[c], mixes.at[c], c_send.at[1], m_recv.at[0], twin).wait_send()
-    remote(ups.at[c], ups.at[c], c_send.at[2], u_recv.at[0], twin).wait_send()
+    face_copy(c, pl.ds(0, height)).wait_send()
 
     @pl.when(is_end)
     def _():
@@ -600,35 +697,39 @@
     terms = term_nodes.shape[0]
     block = (height, width)
     vmem = pl.BlockSpec(memory_space=pltpu.VMEM)
-    smem = pl.BlockSpec(memory_space=pltpu.SMEM)
     dma = pltpu.SemaphoreType.DMA
     count = len(UNITS)
     whole = pltpu.VMEM((2, owned) + block, jnp.float32)
     return pl.pallas_call(
         functools.partial(line_kernel, length, owned, terms),
         out_shape=pltpu.VMEM(meson_nodes.shape, jnp.float32),
-        in_specs=[pl.BlockSpec(memory_space=pl.ANY), smem, smem, smem],
+        in_specs=[pl.BlockSpec(memory_space=pl.ANY)] * 4,
         out_specs=vmem,
-        scratch_shapes=[whole] * 8
+        scratch_shapes=[
+            pltpu.SMEM((2, terms), jnp.int32),
+            pltpu.SMEM(weight_codes.shape, jnp.int32),
+            pltpu.SMEM(resident_pick.shape, jnp.int32),
+        ]
+        + [pltpu.VMEM((2, 2, owned) + block, jnp.float32)] * 2
+        + [whole] * 5
         + [
             pltpu.VMEM((2, 2 * owned, 2) + block, jnp.float32),
             pltpu.VMEM((owned, 2) + block, jnp.float32),
             pltpu.VMEM((owned, 2) + block, jnp.float32),
             pltpu.VMEM((owned, 6, 2, height, width // 2), jnp.bfloat16),
             pltpu.VMEM((owned, 3, 2, 2, height, 3 * width // GROUPS), jnp.bfloat16),
+            pltpu.VMEM((owned, 6, 2) + block, jnp.bfloat16),
             pltpu.VMEM((owned, 4, 2) + block, jnp.bfloat16),
-            pltpu.VMEM((2, owned, 2) + block, jnp.float32),
-            dma((1,)),
+            dma((4,)),
             dma((5,)),
             dma((2, count)),
-            dma((2 * GROUPS,)),
+            dma((GROUPS + 1,)),
             dma((2,)),
             dma((GROUPS,)),
-            dma((len(BATCHES),)),
+            dma((3,)),
             dma((3,)),
             dma((owned,)),
-            dma((len(BATCHES),)),
-            dma((GROUPS + 1,)),
+            dma((len(BATCHES) + 1,)),
             pltpu.SemaphoreType.REGULAR((3,)),
         ],
         compiler_params=pltpu.CompilerParams(

time: 63.2 us -> 61.2 us (0.968)
  Pallas kernels: 62.1 us -> 60 us
    pallas_call x1, Pallas kernels: 62.1 us -> 60 us  [line_body(): pl.pallas_call(functools.partial(line_kernel, length, owned, terms), out_...]
where the time goes in v3:
time: 61.2 us; the launch traced here: 61 us
  Pallas kernels  60 us (98%)
  local copies, waits for them, and re-layouts  0.97 us (2%)
    pallas_call x1, Pallas kernels, line_body(): pl.pallas_call(functools.partial(line_kernel, length, owned, terms), out_...  60 us

profile of v3, /device:TPU:0, one launch (start us, length us, event | category | flops | bytes accessed | tf_op | source)
XLA Modules:
  0.0 61.0 jit_solution(12698944010775988555)
XLA Ops:
  0.0 60.0 %shard_map.46 = f32[2,2,256,256]{3,2,1,0:T(8,128)S(1)} custom-call(f32[2,2,256,256]{3,2,1,0:T(8,128)} %x_ref.1, s32[2,4]{1,0:T(2,128)} %bitcast.1, s32[4]{0:T(128)} %wc_any.1, s32[8]{0:T(128)} %rp_any.1), custom_call_target="tpu_custom_call" | custom-call | tf_op jit(solution)/shard_map/pallas_call | solution.py:703
  60.1 1.0 %copy.6 = f32[2,2,256,256]{3,2,1,0:T(8,128)} copy(f32[2,2,256,256]{3,2,1,0:T(8,128)S(1)} %shard_map.46) | data formatting | bytes 2097152

commit v4 on v3

--- a/solution.py
+++ b/solution.py
@@ -95,10 +95,9 @@
 
 MESH = pl.DeviceIdType.MESH
 UNITS = (2,) * 14 + (1, 1, 1, 1)
-LEADS = (4, 3, 3, 2, 2)
-BATCHES = (2,) * 6 + (1,) * 6
+RAW = 6
+BATCHES = (2,) * 3 + (1,) * 12
 GROUPS = 4
-TAIL = (14, 15, 16, 17)
 
 
 def split(value):
@@ -166,59 +165,87 @@
     return pieces
 
 
-def arrivals_of(pieces):
-    order, sent = [], 0
-    for r in range(len(pieces)):
-        lead = LEADS[r] if r < len(LEADS) else 1
-        while sent < min(r + lead, len(pieces)):
-            order.append((0, sent))
-            sent += 1
-        order.append((1, r))
-    return order
-
-
-def plan_of(order, pieces, height):
-    after = {
-        (0, 1): [("pass", 1), ("right", 0), ("right", 1), ("right", 2), ("right", 3), ("left", 0)],
-        (0, 2): [("pass", 3), ("left", 1)],
-        (1, 0): [("pass", 5), ("facing", 0)],
-        (0, 4): [("pass", 7)],
-        (1, 3): [("pass", 9), ("facing", 1)],
-        (1, 4): [("pass", 11)],
-        (1, 5): [("facing", 2), ("end facing", 3), ("end turn", 0), ("end turn", 1)],
-        (0, 6): [("pass", 13)],
-        (1, 6): [("end turn", 2)],
-        (1, 7): [("mid facing", 3), ("mid turn", 0)],
-        (0, 8): [("pass", 17), ("mid turn", 1), ("mid turn", 2)],
-        (1, 8): [("turn", 3), ("square", 0)],
-        (0, 9): [("square", 1)],
-        (1, 9): [("square", 2)],
-        (0, 10): [("turn", 4), ("square", 3)],
-        (1, 10): [("mine", 0)],
-        (0, 11): [("up", 0)],
-        (1, 11): [("up", 1)],
-        (0, 12): [("turn", 5)],
-        (1, 12): [("up", 2)],
-        (0, 13): [("turn", 6)],
-        (1, 13): [("theirs", 0)],
-        (0, 14): [("turn", 7)],
-        (1, 14): [("up", 3)],
-        (0, 15): [("mine", 1)],
-        (1, 15): [("turn", 8)],
-        (1, 16): [("turn", 9)],
-        (1, 17): [("turn", 10), ("turn", 11), ("late", 0), ("theirs", 1), ("mine", 2), ("up", 4), ("theirs", 2)],
-    }
+def plan_of(role, count):
+    first = list(range(RAW))
+    rest = list(range(RAW, count))
+    order = [("near", p) for p in first] + [("far", p) for p in first]
+    order += [("near", p) for p in rest] + [("far", p) for p in rest]
+    if role == "mid":
+        after = {
+            ("near", 0): [("right", 0), ("right", 1)],
+            ("near", 1): [("pass", 0), ("right", 2), ("right", 3)],
+            ("near", 2): [("left", 0)],
+            ("near", 3): [("pass", 1), ("left", 1)],
+            ("near", 4): [("facing", 0)],
+            ("near", 5): [("pass", 2)],
+            ("far", 1): [("pass", 3)],
+            ("far", 2): [("facing", 1)],
+            ("far", 3): [("pass", 4)],
+            ("far", 5): [("pass", 5)],
+            ("near", 6): [("facing", 2)],
+            ("near", 7): [("pass", 6)],
+            ("near", 9): [("pass", 7)],
+            ("near", 10): [("facing", 3), ("turn", 0)],
+            ("near", 11): [("turn", 1), ("turn", 2)],
+            ("near", 12): [("square", 0), ("square", 1)],
+            ("near", 13): [("square", 2)],
+            ("near", 15): [("square", 3)],
+            ("near", 17): [("square", 4), ("square", 5)],
+            ("far", 6): [("square", 6)],
+            ("far", 7): [("turn", 3), ("square", 7)],
+            ("far", 8): [("turn", 4), ("up", 0)],
+            ("far", 9): [("turn", 5), ("up", 1)],
+            ("far", 10): [("turn", 6)],
+            ("far", 11): [("turn", 7), ("mine", 0)],
+            ("far", 12): [("turn", 8)],
+            ("far", 13): [("turn", 9)],
+            ("far", 14): [("turn", 10)],
+            ("far", 15): [("turn", 11)],
+            ("far", 16): [("turn", 12)],
+            ("far", 17): [
+                ("turn", 13), ("turn", 14), ("theirs", 0), ("up", 2), ("mine", 1), ("up", 3), ("theirs", 1), ("mine", 2),
+                ("up", 4), ("theirs", 2),
+            ],
+        }
+    else:
+        after = {
+            ("near", 0): [("right", 0), ("right", 1), ("right", 2), ("right", 3)],
+            ("near", 1): [("left", 0), ("left", 1)],
+            ("near", 3): [("facing", 0)],
+            ("far", 0): [("facing", 1)],
+            ("far", 4): [("facing", 2)],
+            ("near", 6): [("facing", 3), ("turn", 0), ("turn", 1)],
+            ("near", 7): [("turn", 2)],
+            ("near", 8): [("turn", 3)],
+            ("near", 9): [("turn", 4), ("square", 0)],
+            ("near", 10): [("turn", 5), ("square", 1)],
+            ("near", 11): [("turn", 6), ("square", 2)],
+            ("near", 12): [("turn", 7), ("square", 3)],
+            ("near", 13): [("turn", 8)],
+            ("near", 15): [("turn", 9)],
+            ("near", 17): [("turn", 10), ("turn", 11), ("turn", 12)],
+            ("far", 6): [("turn", 13), ("turn", 14), ("square", 4)],
+            ("far", 7): [("square", 5), ("square", 6)],
+            ("far", 8): [("square", 7), ("up", 0)],
+            ("far", 9): [("up", 1)],
+            ("far", 10): [("mine", 0)],
+            ("far", 11): [("theirs", 0)],
+            ("far", 12): [("mine", 1), ("mine", 2)],
+            ("far", 13): [("up", 2)],
+            ("far", 14): [("theirs", 1)],
+            ("far", 17): [("theirs", 2), ("up", 3), ("up", 4)],
+        }
     plan = []
-    for kind, r in order:
-        plan.append(("far" if kind else "near", r))
-        plan += after.get((kind, r), [])
+    for step in order:
+        plan.append(step)
+        plan += after.get(step, [])
     return plan
 
 
 def line_kernel(
     length, owned, terms,
     x_ref, tn_any, wc_any, rp_any, out_ref,
-    tn_ref, wc_ref, rp_ref, held, faced, outer, inner, far, near_pick, far_pick,
+    tn_ref, wc_ref, rp_ref, held, faced, outer, inner, far, near_pick, far_pick, near_slot, far_slot,
     mixes, turned, turned_far, lefts, packs, rights, squares,
     loc_sem, z_send, z_recv, o_recv, x_send, x_recv, t_recv, c_send, c_recv, m_recv, ready,
 ):
@@ -234,7 +261,6 @@
     height = x_ref.shape[2]
     pieces = pieces_of(height)
     count = len(pieces)
-    order = arrivals_of(pieces)
     group = height // GROUPS
     groups = [(at, group) for at in range(0, height, group)]
     slices = [(0, 2 * group), (2 * group, group), (3 * group, group)]
@@ -244,7 +270,8 @@
         batches.append((pieces[first][0], sum(tall for _, tall in pieces[first : first + size])))
         first += size
     closing = {sum(BATCHES[: k + 1]) - 1: k for k in range(len(BATCHES))}
-    raws = [(0, group // 2), (group // 2, group // 2)] + groups[1:]
+    lifting = {max(p for p, (at, _) in enumerate(pieces) if at < sum(lift)): k for k, lift in enumerate(lifts)}
+    raws = [(at, group // 2) for at in range(0, height, group // 2)]
     low = z < length // 2
     is_end = jnp.logical_or(z == 0, z == length - 1)
     is_mid = jnp.logical_not(is_end)
@@ -277,6 +304,16 @@
             outer.at[:, :, rows(r)], far.at[:, :, rows(r)], z_send.at[2], z_recv.at[1, r], toward_mid
         )
 
+    def near_slot_copy(r):
+        return remote(
+            near_slot.at[:, :, rows(r)], inner.at[:, :, rows(r)], z_send.at[1], z_recv.at[0, r], toward_mid
+        )
+
+    def far_slot_copy(r):
+        return remote(
+            far_slot.at[:, :, rows(r)], far.at[:, :, rows(r)], z_send.at[2], z_recv.at[1, r], toward_mid
+        )
+
     def near_copy(r):
         return remote(
             near_pick.at[:, :, rows(r)], inner.at[:, :, rows(r)], z_send.at[3], z_recv.at[0, r], toward_end
@@ -309,17 +346,13 @@
         part = faced.at[slot, :, :, span]
         return remote(part, part, c_send.at[2], c_recv.at[1], twin)
 
-    tail_span = pl.ds(pieces[TAIL[0]][0], sum(pieces[r][1] for r in TAIL))
-
     def mix_copy(slot, k):
-        span = pl.ds(*batches[k])
-        tail = batches[k][0] >= pieces[TAIL[0]][0]
-        part = mixes.at[slot, pl.ds(owned, owned), :, span] if tail else mixes.at[slot, :, :, span]
+        part = mixes.at[slot, :, pl.ds(owned, owned), pl.ds(*batches[k])]
         return remote(part, part, c_send.at[1], m_recv.at[k], twin)
 
-    def late_copy(slot):
-        part = mixes.at[slot, pl.ds(0, owned), :, tail_span]
-        return remote(part, part, c_send.at[1], m_recv.at[len(batches)], twin)
+    def late_copy(slot, k):
+        part = mixes.at[slot, :, pl.ds(0, owned), pl.ds(*lifts[k])]
+        return remote(part, part, c_send.at[1], m_recv.at[len(batches) + k], twin)
 
     tables = [
         pltpu.make_async_copy(src, dst, loc_sem.at[1 + i])
@@ -351,25 +384,6 @@
         def _():
             pl.semaphore_wait(ready.at[i], 1)
 
-    first_own = order[: order.index((1, 0))]
-    passing = {"sent": len(first_own), "raw": 0}
-
-    def send_until(r):
-        last = order.index((1, r)) + 1
-
-        @pl.when(is_mid)
-        def _():
-            for kind, p in order[passing["sent"] : last]:
-                if kind == 0:
-                    own_copy(p).start()
-                else:
-                    while passing["raw"] == 0 or sum(raws[passing["raw"] - 1]) < sum(pieces[p]):
-                        raw_copy(passing["raw"]).wait_recv()
-                        passing["raw"] += 1
-                    pass_copy(p).start()
-
-        passing["sent"] = last
-
     def open_sends():
         @pl.when(is_end)
         def _():
@@ -378,20 +392,28 @@
 
         @pl.when(is_mid)
         def _():
-            for _, p in first_own:
-                own_copy(p).start()
+            own_copy(0).start()
 
     @pl.when(jnp.logical_not(low))
     def _():
         open_sends()
 
-    meet(0)
-
     @pl.when(low)
     def _():
+        meet(0)
         open_sends()
 
     meet(2)
+
+    @pl.when(is_mid)
+    def _():
+        for p in range(1, RAW):
+            own_copy(p).start()
+
+    @pl.when(jnp.logical_not(low))
+    def _():
+        meet(0)
+
     c_copy(c).start()
     local = pltpu.make_async_copy(x_ref, own, loc_sem.at[0])
     local.start()
@@ -444,27 +466,35 @@
         spot_nodes.append(node)
     home = z * owned
     near_mid = jnp.where(low, z + 1, z - 1) * owned
-    entry_nodes = [home + j for j in range(owned)]
-    entry_nodes += [jnp.where(is_mid, near_mid + j, spot_nodes[j]) for j in range(owned)]
-    entry_nodes += [jnp.where(is_mid, far_end * owned + j, spot_nodes[owned + j]) for j in range(owned)]
-    entry_nodes += [end * owned + j for j in range(owned)]
     zero = jnp.float32(0)
 
-    def weight_of(keys, partners, n, node):
-        total = zero
-        for t in range(terms):
-            match = jnp.logical_and(keys[t] == n, partners[t] == node)
-            total = total + jnp.where(match, factors[t], zero)
-        return total
-
-    def weights_for(base):
+    def slots_of(nodes, consumer):
+        flags = []
+        for node in nodes:
+            flag = jnp.int32(0)
+            for a, b in zip(firsts, seconds):
+                flag = jnp.where(jnp.logical_and(holds(consumer, a), b == node), 1, flag)
+            flags.append(flag)
+        total = sum(flags[1:], flags[0])
+        places = []
+        for i, flag in enumerate(flags):
+            before = sum(flags[:i], jnp.int32(0))
+            places.append(jnp.where(flag == 1, before, total + i - before))
+        return places
+
+    def weights_for(base, nodes):
+        def weight_of(keys, partners, n, node):
+            total = zero
+            for t in range(terms):
+                match = jnp.logical_and(keys[t] == n, partners[t] == node)
+                total = total + jnp.where(match, factors[t], zero)
+            return total
+
         return [
-            [weight_of(keys, partners, base + n, node) for node in entry_nodes]
+            [weight_of(keys, partners, base + n, node) for node in nodes]
             for keys, partners in ((seconds, firsts), (firsts, seconds))
             for n in range(owned)
         ]
-
-    weights, end_weights = weights_for(home), weights_for(end * owned)
 
     def weighted(row, parts):
         total = row[0] * parts[0]
@@ -472,17 +502,11 @@
             total = total + value * part
         return total
 
-    def blend(r, whole, tail=False):
+    def blend(dst, r, table, refs):
         for m in range(2):
-            parts = [ref[m, j, rows(r)] for ref in (own, inner, far) for j in range(owned)]
-            if whole:
-                parts += [outer[m, j, rows(r)] for j in range(owned)]
-            for q, row in enumerate(weights):
-                mixes[c, q, m, rows(r)] = weighted(row, parts)
-            if tail:
-                for q, row in enumerate(end_weights):
-                    dst = far_pick if q < owned else near_pick
-                    dst[m, q % owned, rows(r)] = weighted(row, parts)
+            parts = [ref[m, j, rows(r)] for ref in refs for j in range(owned)]
+            for q, row in enumerate(table):
+                dst[m, q, rows(r)] = weighted(row, parts)
 
     def pick(dst, i, spot, r, sources):
         for m in range(2):
@@ -493,70 +517,94 @@
 
     ranked = [(ref, j) for ref in (own, inner, far) for j in range(owned)]
 
-    def arrive(kind, r):
-        if r in TAIL:
-            return arrive_tail(kind, r)
-
-        @pl.when(is_mid)
-        def _():
-            if kind == 0:
-                own_copy(r).wait_recv()
+    mine = mixes.at[c]
+
+    def close(r, left, right):
+        if right and r in closing:
+            mix_copy(c, closing[r]).start()
+        if left and r in lifting:
+            late_copy(c, lifting[r]).start()
+
+    def mid_actions():
+        raw_nodes = [base + j for base in (near_mid, far_end * owned) for j in range(owned)]
+        known = [home + j for j in range(owned)], [end * owned + j for j in range(owned)]
+        raw_table = weights_for(home, known[0] + raw_nodes + known[1])
+        tables = {}
+
+        def prepare_tables():
+            places = slots_of(raw_nodes, end)
+            nodes = []
+            for i in range(2 * owned):
+                node = jnp.int32(0)
+                for place, name in zip(places, raw_nodes):
+                    node = jnp.where(place == i, name, node)
+                nodes.append(node)
+            tables["own"] = weights_for(home, known[0] + nodes + known[1])
+            tables["end"] = weights_for(end * owned, known[0] + nodes + known[1])
+            tables["places"] = slots_of(known[0] + known[1], far_end)
+
+        def near(r):
+            own_copy(r).wait_recv()
+            if r < RAW:
                 for i in range(owned):
                     pick(near_pick, i, i, r, ranked[: owned + 1 + i])
-                near_copy(r).start()
             else:
-                pass_copy(r).wait_recv()
+                rights_only = [row[: 2 * owned] + row[3 * owned :] for row in tables["end"][owned:]]
+                blend(near_pick, r, rights_only, (own, inner, outer))
+            near_copy(r).start()
+
+        def far_in(r):
+            pass_copy(r).wait_recv()
+            if r < RAW:
                 for i in range(owned):
                     pick(far_pick, i, owned + i, r, ranked[: 2 * owned + 1 + i])
-                far_copy(r).start()
-                blend(r, True)
-
-        @pl.when(is_end)
-        def _():
-            if kind == 0:
-                near_copy(r).wait_recv()
             else:
-                far_copy(r).wait_recv()
-                blend(r, False)
-
-        if kind == 1 and r in closing:
-            mix_copy(c, closing[r]).start()
-
-    def arrive_tail(kind, r):
-        @pl.when(is_mid)
-        def _():
-            if kind == 0:
-                own_copy(r).wait_recv()
+                blend(far_pick, r, tables["end"][:owned], (own, inner, far, outer))
+            far_copy(r).start()
+            blend(mine, r, raw_table if r < RAW else tables["own"], (own, inner, far, outer))
+            close(r, True, True)
+
+        def pass_on(k):
+            raw_copy(k).wait_recv()
+            inside = [p for p, (at, _) in enumerate(pieces) if raws[k][0] <= at < sum(raws[k])]
+            for p in inside:
+                if p < RAW:
+                    pass_copy(p).start()
+                    continue
+                if "places" not in tables:
+                    prepare_tables()
+                for m in range(2):
+                    parts = [ref[m, j, rows(p)] for ref in (own, outer) for j in range(owned)]
+                    for i in range(2 * owned):
+                        chosen = parts[0]
+                        for place, part in zip(tables["places"][1:], parts[1:]):
+                            chosen = jnp.where(place == i, part, chosen)
+                        (near_slot if i < owned else far_slot)[m, i % owned, rows(p)] = chosen
+                near_slot_copy(p).start()
+            if k == len(raws) - 1:
+                for p in range(RAW, count):
+                    far_slot_copy(p).start()
+
+        return {"near": near, "far": far_in, "pass": pass_on}
+
+    def end_actions():
+        table = weights_for(home, [home + j for j in range(owned)] + spot_nodes)
+
+        def near(r):
+            near_copy(r).wait_recv()
+            if r >= RAW:
+                mixes[c, :, owned:, rows(r)] = inner[:, :, rows(r)]
+                close(r, False, True)
+
+        def far_in(r):
+            far_copy(r).wait_recv()
+            if r < RAW:
+                blend(mine, r, table, (own, inner, far))
             else:
-                pass_copy(r).wait_recv()
-                blend(r, True, True)
-                near_copy(r).start()
-                if r > TAIL[0]:
-                    far_copy(r - 1).start()
-                if r == TAIL[-1]:
-                    far_copy(r).start()
-
-        if kind == 1:
-
-            @pl.when(is_end)
-            def _():
-                near_copy(r).wait_recv()
-                for n in range(owned):
-                    for m in range(2):
-                        mixes[c, owned + n, m, rows(r)] = inner[m, n, rows(r)]
-
-            mix_copy(c, closing[r]).start()
-
-    def late(_):
-        @pl.when(is_end)
-        def _():
-            for r in TAIL:
-                far_copy(r).wait_recv()
-                for n in range(owned):
-                    for m in range(2):
-                        mixes[c, n, m, rows(r)] = far[m, n, rows(r)]
-
-        late_copy(c).start()
+                mixes[c, :, :owned, rows(r)] = far[:, :, rows(r)]
+            close(r, True, r < RAW)
+
+        return {"near": near, "far": far_in}
 
     def clear():
         out_ref[...] = jnp.zeros_like(out_ref)
@@ -595,7 +643,7 @@
         return lambda i: rights[n, i].reshape(2 * height, height)
 
     def wide(ref, q, m, span):
-        return jnp.concatenate([ref[h, q, m, span] for h in range(2)], axis=1)
+        return jnp.concatenate([ref[h, m, q, span] for h in range(2)], axis=1)
 
     def turn(k):
         mix_copy(1 - c, k).wait_recv()
@@ -608,20 +656,21 @@
         turned_copy(k).start()
 
     def square(i):
-        n, away = i % owned, i // owned
+        n, quarter = i % owned, i // owned
+        away, at = quarter // 2, quarter % 2 * (height // 2)
         ref, h = (faced, 1 - x) if away else (held, x)
-        if i == owned:
+        if i == 2 * owned:
             face_copy(1 - c, pl.ds(0, height)).wait_recv()
-        left = [jnp.concatenate([ref[h2, m, n] for h2 in range(2)], axis=1) for m in range(2)]
+        span = pl.ds(at, height // 2)
+        left = [jnp.concatenate([ref[h2, m, n, span] for h2 in range(2)], axis=1) for m in range(2)]
         parts = plain_mul(left[0], left[1], right_of(choices[n]))
         for m in range(2):
             for k, part in enumerate(split(parts[m])):
-                squares[n, 2 * m + k, h] = part
+                squares[n, 2 * m + k, h, span] = part
 
     def raise_up(k):
         span = pl.ds(*lifts[k])
-        if k == len(lifts) - 1:
-            late_copy(1 - c).wait_recv()
+        late_copy(1 - c, k).wait_recv()
         for n in range(owned):
             right = lambda i: squares[n, i].reshape(2 * height, height)
             parts = stacked_mul(wide(mixes, n, 0, span), wide(mixes, n, 1, span), right)
@@ -650,28 +699,30 @@
     clear()
     local.wait()
 
-    plan = plan_of(order, pieces, height)
-    actions = {
-        "pass": send_until,
-        "near": lambda r: arrive(0, r),
-        "far": lambda r: arrive(1, r),
-        "late": late,
+    shared = {
         "right": lambda k: put_right(own, x, k),
         "left": prepare_left,
         "facing": prepare_facing,
         "turn": turn,
+        "square": square,
         "up": raise_up,
-        "square": square,
         "mine": lambda k: add_slice(turned, x, k),
         "theirs": add_theirs,
     }
-    for name, i in plan:
-        with jax.named_scope(f"{name}{i}".replace(" ", "_")):
-            where, _, what = name.rpartition(" ")
-            if where:
-                pl.when(is_end if where == "end" else is_mid)(functools.partial(actions[what], i))
-            else:
-                actions[what](i)
+
+    def run(role, own_actions):
+        actions = {**shared, **own_actions()}
+        for name, i in plan_of(role, count):
+            with jax.named_scope(f"{name}{i}"):
+                actions[name](i)
+
+    @pl.when(is_mid)
+    def _():
+        run("mid", mid_actions)
+
+    @pl.when(is_end)
+    def _():
+        run("end", end_actions)
 
     remote(x_ref, facing, x_send.at[0], x_recv.at[0], across).wait_send()
     remote(turned, turned_far, x_send.at[1], t_recv.at[0], across).wait_send()
@@ -711,9 +762,9 @@
             pltpu.SMEM(resident_pick.shape, jnp.int32),
         ]
         + [pltpu.VMEM((2, 2, owned) + block, jnp.float32)] * 2
-        + [whole] * 5
+        + [whole] * 7
         + [
-            pltpu.VMEM((2, 2 * owned, 2) + block, jnp.float32),
+            pltpu.VMEM((2, 2, 2 * owned) + block, jnp.float32),
             pltpu.VMEM((owned, 2) + block, jnp.float32),
             pltpu.VMEM((owned, 2) + block, jnp.float32),
             pltpu.VMEM((owned, 6, 2, height, width // 2), jnp.bfloat16),
@@ -723,13 +774,13 @@
             dma((4,)),
             dma((5,)),
             dma((2, count)),
-            dma((GROUPS + 1,)),
+            dma((2 * GROUPS,)),
             dma((2,)),
             dma((GROUPS,)),
             dma((3,)),
             dma((3,)),
             dma((owned,)),
-            dma((len(BATCHES) + 1,)),
+            dma((len(BATCHES) + GROUPS + 1,)),
             pltpu.SemaphoreType.REGULAR((3,)),
         ],
         compiler_params=pltpu.CompilerParams(

time: 61.2 us -> 57.8 us (0.944)
  Pallas kernels: 60 us -> 56.6 us
    pallas_call x1, Pallas kernels: 60 us -> 56.6 us  [line_body(): pl.pallas_call(functools.partial(line_kernel, length, owned, terms), out_...]
where the time goes in v4:
time: 57.8 us; the launch traced here: 57.6 us
  Pallas kernels  56.6 us (98%)
  local copies, waits for them, and re-layouts  0.97 us (2%)
    pallas_call x1, Pallas kernels, line_body(): pl.pallas_call(functools.partial(line_kernel, length, owned, terms), out_...  56.6 us

profile of v4, /device:TPU:0, one launch (start us, length us, event | category | flops | bytes accessed | tf_op | source)
XLA Modules:
  0.0 57.6 jit_solution(8179271047954728202)
XLA Ops:
  0.0 56.6 %shard_map.46 = f32[2,2,256,256]{3,2,1,0:T(8,128)S(1)} custom-call(f32[2,2,256,256]{3,2,1,0:T(8,128)} %x_ref.1, s32[2,4]{1,0:T(2,128)} %bitcast.1, s32[4]{0:T(128)} %wc_any.1, s32[8]{0:T(128)} %rp_any.1), custom_call_target="tpu_custom_call" | custom-call | tf_op jit(solution)/shard_map/pallas_call | solution.py:754
  56.6 1.0 %copy.6 = f32[2,2,256,256]{3,2,1,0:T(8,128)} copy(f32[2,2,256,256]{3,2,1,0:T(8,128)S(1)} %shard_map.46) | data formatting | bytes 2097152

commit v5 on v4

--- a/solution.py
+++ b/solution.py
@@ -96,7 +96,7 @@
 MESH = pl.DeviceIdType.MESH
 UNITS = (2,) * 14 + (1, 1, 1, 1)
 RAW = 6
-BATCHES = (2,) * 3 + (1,) * 12
+BATCHES = (2,) * 3 + (1,) * 8 + (2, 1, 1)
 GROUPS = 4
 
 
@@ -200,10 +200,8 @@
             ("far", 12): [("turn", 8)],
             ("far", 13): [("turn", 9)],
             ("far", 14): [("turn", 10)],
-            ("far", 15): [("turn", 11)],
-            ("far", 16): [("turn", 12)],
             ("far", 17): [
-                ("turn", 13), ("turn", 14), ("theirs", 0), ("up", 2), ("mine", 1), ("up", 3), ("theirs", 1), ("mine", 2),
+                ("turn", 11), ("turn", 12), ("turn", 13), ("theirs", 0), ("up", 2), ("mine", 1), ("up", 3), ("theirs", 1), ("mine", 2),
                 ("up", 4), ("theirs", 2),
             ],
         }
@@ -223,8 +221,8 @@
             ("near", 12): [("turn", 7), ("square", 3)],
             ("near", 13): [("turn", 8)],
             ("near", 15): [("turn", 9)],
-            ("near", 17): [("turn", 10), ("turn", 11), ("turn", 12)],
-            ("far", 6): [("turn", 13), ("turn", 14), ("square", 4)],
+            ("near", 17): [("turn", 10), ("turn", 11)],
+            ("far", 6): [("turn", 12), ("turn", 13), ("square", 4)],
             ("far", 7): [("square", 5), ("square", 6)],
             ("far", 8): [("square", 7), ("up", 0)],
             ("far", 9): [("up", 1)],
@@ -270,7 +268,9 @@
         batches.append((pieces[first][0], sum(tall for _, tall in pieces[first : first + size])))
         first += size
     closing = {sum(BATCHES[: k + 1]) - 1: k for k in range(len(BATCHES))}
-    lifting = {max(p for p, (at, _) in enumerate(pieces) if at < sum(lift)): k for k, lift in enumerate(lifts)}
+    last = pieces[-1]
+    shares = lifts[:-1] + [(lifts[-1][0], lifts[-1][1] - last[1]), last]
+    lifting = {max(p for p, (at, _) in enumerate(pieces) if at < sum(share)): k for k, share in enumerate(shares)}
     raws = [(at, group // 2) for at in range(0, height, group // 2)]
     low = z < length // 2
     is_end = jnp.logical_or(z == 0, z == length - 1)
@@ -351,7 +351,7 @@
         return remote(part, part, c_send.at[1], m_recv.at[k], twin)
 
     def late_copy(slot, k):
-        part = mixes.at[slot, :, pl.ds(0, owned), pl.ds(*lifts[k])]
+        part = mixes.at[slot, :, pl.ds(0, owned), pl.ds(*shares[k])]
         return remote(part, part, c_send.at[1], m_recv.at[len(batches) + k], twin)
 
     tables = [
@@ -671,6 +671,8 @@
     def raise_up(k):
         span = pl.ds(*lifts[k])
         late_copy(1 - c, k).wait_recv()
+        if k == len(lifts) - 1:
+            late_copy(1 - c, k + 1).wait_recv()
         for n in range(owned):
             right = lambda i: squares[n, i].reshape(2 * height, height)
             parts = stacked_mul(wide(mixes, n, 0, span), wide(mixes, n, 1, span), right)
@@ -780,7 +782,7 @@
             dma((3,)),
             dma((3,)),
             dma((owned,)),
-            dma((len(BATCHES) + GROUPS + 1,)),
+            dma((len(BATCHES) + GROUPS + 2,)),
             pltpu.SemaphoreType.REGULAR((3,)),
         ],
         compiler_params=pltpu.CompilerParams(

time: 57.8 us -> 57.7 us (level)
  no operation moved by 1% of the time
where the time goes in v5:
time: 57.7 us; the launch traced here: 57.6 us
  Pallas kernels  56.6 us (98%)
  local copies, waits for them, and re-layouts  0.97 us (2%)
    pallas_call x1, Pallas kernels, line_body(): pl.pallas_call(functools.partial(line_kernel, length, owned, terms), out_...  56.6 us

profile of v5, /device:TPU:0, one launch (start us, length us, event | category | flops | bytes accessed | tf_op | source)
XLA Modules:
  0.0 57.6 jit_solution(3997649486254829201)
XLA Ops:
  0.0 56.6 %shard_map.46 = f32[2,2,256,256]{3,2,1,0:T(8,128)S(1)} custom-call(f32[2,2,256,256]{3,2,1,0:T(8,128)} %x_ref.1, s32[2,4]{1,0:T(2,128)} %bitcast.1, s32[4]{0:T(128)} %wc_any.1, s32[8]{0:T(128)} %rp_any.1), custom_call_target="tpu_custom_call" | custom-call | tf_op jit(solution)/shard_map/pallas_call | solution.py:756
  56.6 1.0 %copy.6 = f32[2,2,256,256]{3,2,1,0:T(8,128)} copy(f32[2,2,256,256]{3,2,1,0:T(8,128)S(1)} %shard_map.46) | data formatting | bytes 2097152

commit v6 on v5

--- a/solution.py
+++ b/solution.py
@@ -96,7 +96,7 @@
 MESH = pl.DeviceIdType.MESH
 UNITS = (2,) * 14 + (1, 1, 1, 1)
 RAW = 6
-BATCHES = (2,) * 3 + (1,) * 8 + (2, 1, 1)
+BATCHES = (2,) * 3 + (1,) * 12
 GROUPS = 4
 
 
@@ -200,8 +200,10 @@
             ("far", 12): [("turn", 8)],
             ("far", 13): [("turn", 9)],
             ("far", 14): [("turn", 10)],
+            ("far", 15): [("turn", 11)],
+            ("far", 16): [("turn", 12)],
             ("far", 17): [
-                ("turn", 11), ("turn", 12), ("turn", 13), ("theirs", 0), ("up", 2), ("mine", 1), ("up", 3), ("theirs", 1), ("mine", 2),
+                ("turn", 13), ("turn", 14), ("theirs", 0), ("up", 2), ("mine", 1), ("up", 3), ("theirs", 1), ("mine", 2),
                 ("up", 4), ("theirs", 2),
             ],
         }
@@ -221,8 +223,8 @@
             ("near", 12): [("turn", 7), ("square", 3)],
             ("near", 13): [("turn", 8)],
             ("near", 15): [("turn", 9)],
-            ("near", 17): [("turn", 10), ("turn", 11)],
-            ("far", 6): [("turn", 12), ("turn", 13), ("square", 4)],
+            ("near", 17): [("turn", 10), ("turn", 11), ("turn", 12)],
+            ("far", 6): [("turn", 13), ("turn", 14), ("square", 4)],
             ("far", 7): [("square", 5), ("square", 6)],
             ("far", 8): [("square", 7), ("up", 0)],
             ("far", 9): [("up", 1)],
@@ -296,32 +298,32 @@
 
     def own_copy(r):
         return remote(
-            x_ref.at[:, :, rows(r)], inner.at[:, :, rows(r)], z_send.at[1], z_recv.at[0, r], toward_mid
+            x_ref.at[:, :, rows(r)], inner.at[:, :, rows(r)], z_send.at[0], z_recv.at[0, r], toward_mid
         )
 
     def pass_copy(r):
         return remote(
-            outer.at[:, :, rows(r)], far.at[:, :, rows(r)], z_send.at[2], z_recv.at[1, r], toward_mid
+            outer.at[:, :, rows(r)], far.at[:, :, rows(r)], z_send.at[1], z_recv.at[1, r], toward_mid
         )
 
     def near_slot_copy(r):
         return remote(
-            near_slot.at[:, :, rows(r)], inner.at[:, :, rows(r)], z_send.at[1], z_recv.at[0, r], toward_mid
+            near_slot.at[:, :, rows(r)], inner.at[:, :, rows(r)], z_send.at[0], z_recv.at[0, r], toward_mid
         )
 
     def far_slot_copy(r):
         return remote(
-            far_slot.at[:, :, rows(r)], far.at[:, :, rows(r)], z_send.at[2], z_recv.at[1, r], toward_mid
+            far_slot.at[:, :, rows(r)], far.at[:, :, rows(r)], z_send.at[1], z_recv.at[1, r], toward_mid
         )
 
     def near_copy(r):
         return remote(
-            near_pick.at[:, :, rows(r)], inner.at[:, :, rows(r)], z_send.at[3], z_recv.at[0, r], toward_end
+            near_pick.at[:, :, rows(r)], inner.at[:, :, rows(r)], z_send.at[2], z_recv.at[0, r], toward_end
         )
 
     def far_copy(r):
         return remote(
-            far_pick.at[:, :, rows(r)], far.at[:, :, rows(r)], z_send.at[4], z_recv.at[1, r], toward_end
+            far_pick.at[:, :, rows(r)], far.at[:, :, rows(r)], z_send.at[3], z_recv.at[1, r], toward_end
         )
 
     def x_copy(k):
@@ -738,10 +740,10 @@
 
     @pl.when(is_mid)
     def _():
-        remote(x_ref, inner, z_send.at[1], z_recv.at[0, 0], toward_mid).wait_send()
-        remote(outer, far, z_send.at[2], z_recv.at[1, 0], toward_mid).wait_send()
-        remote(near_pick, inner, z_send.at[3], z_recv.at[0, 0], toward_end).wait_send()
-        remote(far_pick, far, z_send.at[4], z_recv.at[1, 0], toward_end).wait_send()
+        remote(x_ref, inner, z_send.at[0], z_recv.at[0, 0], toward_mid).wait_send()
+        remote(outer, far, z_send.at[1], z_recv.at[1, 0], toward_mid).wait_send()
+        remote(near_pick, inner, z_send.at[2], z_recv.at[0, 0], toward_end).wait_send()
+        remote(far_pick, far, z_send.at[3], z_recv.at[1, 0], toward_end).wait_send()
 
 
 def line_body(meson_nodes, term_nodes, weight_codes, resident_pick):
@@ -774,7 +776,7 @@
             pltpu.VMEM((owned, 6, 2) + block, jnp.bfloat16),
             pltpu.VMEM((owned, 4, 2) + block, jnp.bfloat16),
             dma((4,)),
-            dma((5,)),
+            dma((4,)),
             dma((2, count)),
             dma((2 * GROUPS,)),
             dma((2,)),

time: 57.7 us -> 57.7 us (level)
  no operation moved by 1% of the time
where the time goes in v6:
time: 57.7 us; the launch traced here: 57.6 us
  Pallas kernels  56.6 us (98%)
  local copies, waits for them, and re-layouts  0.97 us (2%)
    pallas_call x1, Pallas kernels, line_body(): pl.pallas_call(functools.partial(line_kernel, length, owned, terms), out_...  56.6 us

profile of v6, /device:TPU:0, one launch (start us, length us, event | category | flops | bytes accessed | tf_op | source)
XLA Modules:
  0.0 57.6 jit_solution(12862351323249059510)
XLA Ops:
  0.0 56.6 %shard_map.46 = f32[2,2,256,256]{3,2,1,0:T(8,128)S(1)} custom-call(f32[2,2,256,256]{3,2,1,0:T(8,128)} %x_ref.1, s32[2,4]{1,0:T(2,128)} %bitcast.1, s32[4]{0:T(128)} %wc_any.1, s32[8]{0:T(128)} %rp_any.1), custom_call_target="tpu_custom_call" | custom-call | tf_op jit(solution)/shard_map/pallas_call | solution.py:758
  56.6 1.0 %copy.6 = f32[2,2,256,256]{3,2,1,0:T(8,128)} copy(f32[2,2,256,256]{3,2,1,0:T(8,128)S(1)} %shard_map.46) | data formatting | bytes 2097152
